TPU v7x, 256 devices: a whole 4x4x8 slice. The times are simulated.
256 devices in a mesh: frame: 64 (over y, x_hi, z), clip: 4 (over x_lo, core).
Axes of the slice: x: 4 (x_hi: 2, x_lo: 2; x = x_hi * 2 + x_lo), y: 4, z: 8, core: 2. Of those that a mesh axis runs over, the one named last changes fastest.
Arguments:
- tokens: bfloat16 [4, 512, 2, 49, 256], P('clip', 'frame'), may hold values from -6 to 6
- lengths: int32 [4], P('clip'), may hold values from 256 to 512, as said below
- norm_gain: float32 [256], replicated, may hold values from 0.25 to 1.75
- norm_bias: float32 [256], replicated, may hold values from -1.5 to 1.5
- qkv_weight: float32 [256, 768], replicated, may hold values from -0.375 to 0.375
- qkv_bias: float32 [768], replicated, may hold values from -1.5 to 1.5
- proj_weight: float32 [256, 256], replicated, may hold values from -0.375 to 0.375
- proj_bias: float32 [256], replicated, may hold values from -1.5 to 1.5
- grad_out: bfloat16 [4, 512, 2, 49, 256], P('clip', 'frame'), may hold values from -6 to 6
Outputs:
- mixed: bfloat16 [4, 512, 2, 49, 256], P('clip', 'frame')
- grad_tokens: bfloat16 [4, 512, 2, 49, 256], P('clip', 'frame')
- grad_gain: float32 [256], replicated
- grad_nbias: float32 [256], replicated
- grad_qkv_weight: float32 [256, 768], replicated
- grad_qkv_bias: float32 [768], replicated
- grad_proj_weight: float32 [256, 256], replicated
- grad_proj_bias: float32 [256], replicated
Inputs may be any that keep to these rules, and one draw needn't show every extreme that they name: `lengths`: each clip has at least 256 frames that are not padding, and at least one clip has all 512 frames.
All inputs are finite; a program needn't handle non-finite values.
Results may differ from a plain program's by a relative error of at most 0.012.
Values may be sent and summed in bfloat16 or wider, within the bound.
No kernel may reach another device: no remote copies, remote signals or barrier semaphores. Data moves between devices by JAX's collectives and lax.ppermute only.
A program may use at most 192 MiB of HBM per device.

v0:
```python
import jax
import jax.numpy as jnp
from jax import lax
from jax.sharding import PartitionSpec as P

HEADS = 8
WT = 8


def passed_along(array, axis, by):
    devices = lax.axis_size(axis)
    return lax.ppermute(array, axis, [(i, (i + by) % devices) for i in range(devices)])


def branch(
    slab,
    length,
    first_frame,
    frame_total,
    norm_gain,
    norm_bias,
    qkv_weight,
    qkv_bias,
    proj_weight,
    proj_bias,
):
    frames, windows, patch_len, model_width = slab.shape
    head_count = HEADS
    head_depth = model_width // head_count
    offset = WT // 2
    frame_index = jnp.mod(first_frame + jnp.arange(frames, dtype=jnp.int32), frame_total)
    valid_frame = frame_index < length
    region = frame_index < offset
    values = slab.astype(jnp.float32)
    mean_val = jnp.mean(values, axis=-1, keepdims=True)
    variance = jnp.mean((values - mean_val) ** 2, axis=-1, keepdims=True)
    normed = ((values - mean_val) * lax.rsqrt(variance + 1e-05) * norm_gain + norm_bias).astype(
        jnp.bfloat16
    )
    project_qkv = (
        jnp.dot(
            normed.reshape(-1, model_width),
            qkv_weight.astype(jnp.bfloat16),
            preferred_element_type=jnp.float32,
        )
        + qkv_bias
    )
    project_qkv = project_qkv.astype(jnp.bfloat16)
    time_windows = frames // WT
    project_qkv = project_qkv.reshape(
        time_windows, WT, windows, patch_len, 3, head_count, head_depth
    )
    project_qkv = project_qkv.transpose(4, 0, 2, 5, 1, 3, 6).reshape(
        3, time_windows, windows, head_count, WT * patch_len, head_depth
    )
    queries = project_qkv[0].astype(jnp.float32)
    keys_f = project_qkv[1].astype(jnp.float32)
    values_f = project_qkv[2].astype(jnp.float32)
    key_valid = jnp.repeat(valid_frame.reshape(time_windows, WT), patch_len, axis=1)
    key_region = jnp.repeat(region.reshape(time_windows, WT), patch_len, axis=1)
    allowed = key_valid[:, None, :] & (key_region[:, :, None] == key_region[:, None, :])
    scores = jnp.einsum("nwhqe,nwhke->nwhqk", queries, keys_f) * head_depth ** (-0.5)
    scores = jnp.where(allowed[:, None, None], scores, -1000000000.0)
    attn_probs = jax.nn.softmax(scores, axis=-1).astype(jnp.bfloat16)
    attended = jnp.einsum("nwhqk,nwhke->nwhqe", attn_probs.astype(jnp.float32), values_f).astype(
        jnp.bfloat16
    )
    attended = attended.reshape(time_windows, windows, head_count, WT, patch_len, head_depth)
    attended = attended.transpose(0, 3, 1, 4, 2, 5).reshape(-1, model_width)
    projected = (
        jnp.dot(attended, proj_weight.astype(jnp.bfloat16), preferred_element_type=jnp.float32)
        + proj_bias
    )
    projected = (
        projected.reshape(frames, windows, patch_len, model_width)
        * valid_frame.astype(jnp.float32)[:, None, None, None]
    )
    return projected.astype(jnp.bfloat16)


def per_device(
    tokens, lengths, norm_gain, norm_bias, qkv_weight, qkv_bias, proj_weight, proj_bias, grad_out
):
    frames_dev = tokens.shape[1]
    offset = WT // 2
    frame_total = frames_dev * lax.axis_size("frame")
    first_frame = lax.axis_index("frame") * frames_dev
    length = lengths[0]
    params = (norm_gain, norm_bias, qkv_weight, qkv_bias, proj_weight, proj_bias)
    ahead_rows = passed_along(tokens[:, :offset], "frame", -1)
    rolled = jnp.concatenate([tokens[:, offset:], ahead_rows], axis=1)

    def local_fn(slab_in, param_set):
        return branch(slab_in[0], length, first_frame + offset, frame_total, *param_set)[None]

    branch_out, pullback = jax.vjp(local_fn, rolled, params)
    behind = passed_along(branch_out[:, frames_dev - offset :], "frame", 1)
    branch_own = jnp.concatenate([behind, branch_out[:, : frames_dev - offset]], axis=1)
    ahead_grad = passed_along(grad_out[:, :offset], "frame", -1)
    grad_rolled_in = jnp.concatenate([grad_out[:, offset:], ahead_grad], axis=1)
    grad_rolled, grad_params = pullback(grad_rolled_in)
    back_rows = passed_along(grad_rolled[:, frames_dev - offset :], "frame", 1)
    grad_tokens = grad_out + jnp.concatenate(
        [back_rows, grad_rolled[:, : frames_dev - offset]], axis=1
    )
    mixed = (tokens.astype(jnp.float32) + branch_own.astype(jnp.float32)).astype(jnp.bfloat16)
    grad_gain, grad_nbias, grad_qkv_w, grad_qkv_b, grad_proj_w, grad_proj_b = grad_params
    summed = lax.psum(
        (grad_gain, grad_nbias, grad_qkv_w, grad_qkv_b, grad_proj_w, grad_proj_b), ("frame", "clip")
    )
    return (mixed, grad_tokens, summed[0], summed[1], summed[2], summed[3], summed[4], summed[5])


def solution(mesh):
    in_specs = (
        P("clip", "frame", None, None, None),
        P("clip"),
        P(),
        P(),
        P(),
        P(),
        P(),
        P(),
        P("clip", "frame", None, None, None),
    )
    out_specs = (
        P("clip", "frame", None, None, None),
        P("clip", "frame", None, None, None),
        P(),
        P(),
        P(),
        P(),
        P(),
        P(),
    )
    return jax.shard_map(
        per_device, mesh=mesh, in_specs=in_specs, out_specs=out_specs, check_vma=False
    )
```

profile of v0, /device:TPU:1, one launch (start us, length us, event | category | flops | bytes accessed | tf_op | source)
XLA Modules:
  0.0 429.6 jit_solution(4308741729636030882)
XLA Ops:
  7.2 1.3 fusion.43
  8.6 11.4 %collective-permute-start = (bf16[1,4,2,49,256]{4,3,2,1,0:T(8,128)(2,1)S(1)}, bf16[1,4,2,49,256]{4,3,2,1,0:T(8,128)(2,1)S(1)}, u32[]{:S(2)}, u32[]{:S(2)}) collective-permute-start(bf16[1,4,2,49,256]{4,3,2,1,0:T(8,128)(2,1)S(1)} %copy.79), channel_id=1, source_target_pairs={{0,252},{4,0},{8,4},{12,8},{16,12},{20,16},{24,20},{28,24},{32,28}... | collective-permute-start | bytes 602120 | tf_op jit(solution)/shard_map/ppermute | solution.py:12
  20.0 1.3 fusion.42
  21.3 0.8 collective-permute-start.2
  23.4 0.9 compare_and_fusion
  26.4 1.0 reshape.586
  27.4 2.0 add_convert_fusion
  29.4 1.8 copy.52
  31.2 1.0 broadcast_multiply_fusion
  32.9 1.7 reshape.582
  34.9 1.5 reshape.583
  36.4 12.6 %reshape.575 = bf16[1,8,2,49,3,8,32]{3,2,1,6,5,4,0:T(2,128)(2,1)S(1)} reshape(bf16[784,768]{0,1:T(8,128)(2,1)} %copy.52) | data formatting | bytes 2408448 | tf_op jit(solution)/shard_map/jvp()/reshape | solution.py:50
  49.0 3.3 fusion.39
  53.2 1.4 copy.54
  55.3 1.5 copy.53
  57.5 8.4 %fusion.44 = (f32[2,8,392]{2,1,0:T(8,128)S(1)}, f32[2,8,392,392]{2,3,1,0:T(8,128)}) fusion(pred[392,392]{0,1:T(8,128)(4,1)} %compare_and_fusion, bf16[2,8,392,32]{2,3,1,0:T(8,128)(2,1)S(1)} %reshape.576, bf16[2,8,392,32]{2,3,1,0:T(8,128)(2,1)S(1)} %reshape.577), kind=kOutput, calls=%fused_computation.88 | convolution fusion | flops 167186816 | bytes 10816064 | tf_op jit(solution)/shard_map/jvp()/sub | solution.py:64
  66.0 9.2 %fusion.6 = (f32[2,8,392]{2,1,0:T(8,128)S(1)}, bf16[2,8,392,392]{2,3,1,0:T(8,128)(2,1)}, bf16[2,8,392,392]{2,3,1,0:T(8,128)(2,1)}) fusion(f32[2,8,392,392]{2,3,1,0:T(8,128)} %get-tuple-element.56, f32[2,8,392]{2,1,0:T(8,128)S(1)} %multiply_divide_fusion, f32[2,8,392]{2,1,0:T(8,128)S(1)} %get-tuple-element.55, bf16[2,8,392,32]{2,3,1,0:T(8,128)(2,1)S(1)} %copy-done.2, ...), kind=kOutput, calls=%fused_computation.8 | convolution fusion | flops 174556032 | bytes 20547072 | tf_op jit(solution)/shard_map/transpose(jvp(nwhqk,nwhke->nwhqe))/dot_general | solution.py:65
  75.3 9.9 %fusion.16 = bf16[1,1,2,8,392,32]{4,5,3,2,1,0:T(8,128)(2,1)S(1)} fusion(bf16[2,8,392,32]{2,3,1,0:T(8,128)(2,1)S(1)} %reshape.577, f32[2,8,392,392]{2,3,1,0:T(8,128)} %get-tuple-element.56, bf16[2,8,392,392]{2,3,1,0:T(8,128)(2,1)} %get-tuple-element.57, f32[2,8,392]{2,1,0:T(8,128)S(1)} %neg.15, f32[2,8,392]{2,1,0:T(8,128)S(1)} %get-tuple-element.55, ...), kind=kOutput, calls=%fused_computation.33 | convolution fusion | flops 172304384 | bytes 15758400 | tf_op jit(solution)/shard_map/transpose(jvp(nwhqe,nwhke->nwhqk))/dot_general | solution.py:62
  85.2 8.4 %fusion.15 = bf16[1,1,2,8,392,32]{4,5,3,2,1,0:T(8,128)(2,1)S(1)} fusion(bf16[2,8,392,32]{2,3,1,0:T(8,128)(2,1)S(1)} %reshape.576, f32[2,8,392,392]{2,3,1,0:T(8,128)} %get-tuple-element.56, bf16[2,8,392,392]{2,3,1,0:T(8,128)(2,1)} %get-tuple-element.57, f32[2,8,392]{2,1,0:T(8,128)S(1)} %neg.15, f32[2,8,392]{2,1,0:T(8,128)S(1)} %get-tuple-element.55, ...), kind=kOutput, calls=%fused_computation.32 | convolution fusion | flops 172304384 | bytes 15758400 | tf_op jit(solution)/shard_map/transpose(jvp(nwhqe,nwhke->nwhqk))/dot_general | solution.py:62
  93.6 4.7 %fusion.17 = bf16[1,1,2,8,392,32]{4,5,3,2,1,0:T(8,128)(2,1)S(1)} fusion(bf16[2,8,392,32]{2,3,1,0:T(8,128)(2,1)S(1)} %copy-done.2, bf16[2,8,392,392]{2,3,1,0:T(8,128)(2,1)} %get-tuple-element.37), kind=kOutput, calls=%fused_computation.34 | convolution fusion | flops 157552640 | bytes 5720064 | tf_op jit(solution)/shard_map/transpose(jvp(nwhqk,nwhke->nwhqe))/dot_general | solution.py:65
  98.3 4.8 %convolution_convert_fusion.2 = bf16[2,8,392,32]{2,3,1,0:T(8,128)(2,1)} fusion(bf16[2,8,392,392]{2,3,1,0:T(8,128)(2,1)} %get-tuple-element.37, bf16[2,8,392,32]{2,3,1,0:T(8,128)(2,1)S(1)} %reshape.578), kind=kOutput, calls=%fused_computation.24 | convolution fusion | flops 157552640 | bytes 5720064 | tf_op jit(solution)/shard_map/jvp(nwhqk,nwhke->nwhqe)/dot_general | solution.py:65
  103.0 1.3 pad_add_fusion
  104.4 5.2 %reshape.584 = bf16[3,1,2,8,8,49,32]{5,4,6,3,2,0,1:T(8,128)(2,1)S(1)} reshape(bf16[3,1,2,8,392,32]{4,5,3,2,1,0:T(8,128)(2,1)} %pad_add_fusion) | data formatting | bytes 2408448 | tf_op jit(solution)/shard_map/transpose(jvp())/reshape | solution.py:53
  109.6 6.8 %convert_reduce_fusion = f32[3,8,32]{2,1,0:T(8,128)} fusion(bf16[3,1,2,8,8,49,32]{5,4,6,3,2,0,1:T(8,128)(2,1)S(1)} %reshape.584), kind=kLoop, calls=%fused_computation.16 | loop fusion | flops 1203456 | bytes 1207296 | tf_op jit(solution)/shard_map/transpose(jvp())/reduce_sum | solution.py:41
  116.4 6.6 %copy.83 = bf16[3,1,2,8,8,49,32]{5,2,4,6,3,0,1:T(2,128)(2,1)} copy(bf16[3,1,2,8,8,49,32]{5,4,6,3,2,0,1:T(8,128)(2,1)S(1)} %reshape.584) | data formatting | bytes 2408448 | tf_op jit(solution)/shard_map/transpose(jvp())/reshape | solution.py:53
  122.9 10.1 %reshape.585 = bf16[784,768]{0,1:T(8,128)(2,1)S(1)} reshape(bf16[1,8,2,49,3,8,32]{3,2,1,6,5,4,0:T(2,128)(2,1)} %bitcast.83) | data formatting | bytes 2408448 | tf_op jit(solution)/shard_map/transpose(jvp())/reshape | solution.py:50
  133.0 2.4 fusion.37
  135.5 1.1 reshape.589
  136.5 1.1 reshape.588
  137.6 1.2 mul.259
  138.7 2.1 reshape.579
  140.9 2.6 copy.84
  143.5 4.0 reshape.580
  147.4 1.0 fusion.18
  148.5 1.2 convolution_add_fusion
  149.8 1.9 fusion.33
  151.8 0.8 fusion.41
  154.1 2.3 multiply_reduce_fusion
  157.1 1.2 multiply_reduce_fusion.1
  158.3 2.0 add_convert_fusion.1
  160.4 1.5 fusion.14
  162.8 78.9 %all-reduce.3 = (f32[256]{0:T(256)}, f32[256]{0:T(256)}, f32[768]{0:T(1024)}, f32[256]{0:T(256)}) all-reduce(f32[256]{0:T(256)} %get-tuple-element.24, f32[256]{0:T(256)} %get-tuple-element.26, f32[768]{0:T(1024)S(1)} %reduce_sum.118, f32[256]{0:T(256)} %get-tuple-element.53), channel_id=1, replica_groups=mesh['frame'=64,'clip'=4] {'frame','clip'}, use_global_device_ids=true, to_apply=%region_9.10 | all-reduce | flops 1536 | bytes 12288 | tf_op jit(solution)/shard_map/psum | solution.py:108
  241.7 1.3 add_convert_fusion.3
  243.0 1.1 copy.67
  244.2 1.1 copy.68
  245.3 173.5 %all-reduce.7.cloned.1.call-done = (f32[256,768]{1,0:T(8,128)}, f32[256,256]{1,0:T(8,128)}) async-done(((f32[256,768]{1,0:T(8,128)}, f32[256,256]{1,0:T(8,128)}), (f32[256,768]{1,0:T(8,128)}, f32[256,256]{1,0:T(8,128)})) %all-reduce.7.cloned.1.call-update) | async-done | bytes 1048592 | tf_op jit(solution)/shard_map/psum | solution.py:108
  418.8 2.1 copy.88
  420.8 1.7 copy.89
  (72 shorter events, 9.4 us)
Async XLA Ops:
  7.2 25.2 %copy-start.5 = (f32[256,256]{1,0:T(8,128)S(1)}, f32[256,256]{1,0:T(8,128)}, u32[]{:S(2)}) copy-start(f32[256,256]{1,0:T(8,128)} %param.15) | copy-start | bytes 786436
  7.2 411.6 %all-reduce.7.cloned.1.call-start = ((), (), s32[]{:S(2)}) async-start(), calls=%async_computation | async-start | bytes 2097152 | tf_op jit(solution)/shard_map/psum | solution.py:108
  8.6 15.7 %collective-permute-start = (bf16[1,4,2,49,256]{4,3,2,1,0:T(8,128)(2,1)S(1)}, bf16[1,4,2,49,256]{4,3,2,1,0:T(8,128)(2,1)S(1)}, u32[]{:S(2)}, u32[]{:S(2)}) collective-permute-start(bf16[1,4,2,49,256]{4,3,2,1,0:T(8,128)(2,1)S(1)} %copy.79), channel_id=1, source_target_pairs={{0,252},{4,0},{8,4},{12,8},{16,12},{20,16},{24,20},{28,24},{32,28}... | collective-permute-start | bytes 602120 | tf_op jit(solution)/shard_map/ppermute | solution.py:12
  21.3 9.9 %collective-permute-start.2 = (bf16[1,4,2,49,256]{4,3,2,1,0:T(8,128)(2,1)S(1)}, bf16[1,4,2,49,256]{4,3,2,1,0:T(8,128)(2,1)S(1)}, u32[]{:S(2)}, u32[]{:S(2)}) collective-permute-start(bf16[1,4,2,49,256]{4,3,2,1,0:T(8,128)(2,1)S(1)} %copy.81), channel_id=1, source_target_pairs={{0,252},{4,0},{8,4},{12,8},{16,12},{20,16},{24,20},{28,24},{32,28}... | collective-permute-start | bytes 602120 | tf_op jit(solution)/shard_map/ppermute | solution.py:12
  22.8 26.1 %copy-start.12 = (f32[8]{0:T(128)}, f32[8]{0:T(128)S(1)}, u32[]{:S(2)}) copy-start(f32[8]{0:T(128)S(1)} %get-tuple-element.34) | copy-start | bytes 100
  23.4 8.8 %copy-start.3 = (bf16[1,4,2,49,256]{4,3,2,1,0:T(8,128)(2,1)}, bf16[1,4,2,49,256]{4,3,2,1,0:T(8,128)(2,1)S(1)}, u32[]{:S(2)}) copy-start(bf16[1,4,2,49,256]{4,3,2,1,0:T(8,128)(2,1)S(1)} %copy.82) | copy-start | bytes 602116
  24.3 10.5 %copy-start = (bf16[1,4,2,49,256]{4,3,2,1,0:T(8,128)(2,1)}, bf16[1,4,2,49,256]{4,3,2,1,0:T(8,128)(2,1)S(1)}, u32[]{:S(2)}) copy-start(bf16[1,4,2,49,256]{4,3,2,1,0:T(8,128)(2,1)S(1)} %collective-permute-done) | copy-start | bytes 602116
  24.5 0.6 copy-start.7
  25.0 0.6 copy-start.10
  25.6 0.6 copy-start.9
  31.2 3.7 copy-start.6
  55.3 10.7 %copy-start.2 = (bf16[2,8,392,32]{2,3,1,0:T(8,128)(2,1)S(1)}, bf16[2,8,392,32]{2,3,1,0:T(8,128)(2,1)}, u32[]{:S(2)}) copy-start(bf16[2,8,392,32]{2,3,1,0:T(8,128)(2,1)} %reshape.583) | copy-start | bytes 1204228
  66.0 9.3 %copy-start.8 = (pred[392,392]{0,1:T(8,128)(4,1)S(1)}, pred[392,392]{0,1:T(8,128)(4,1)}, u32[]{:S(2)}) copy-start(pred[392,392]{0,1:T(8,128)(4,1)} %compare_and_fusion) | copy-start | bytes 460996
  98.3 34.8 %copy-start.11 = (f32[256]{0:T(256)S(1)}, f32[256]{0:T(256)}, u32[]{:S(2)}) copy-start(f32[256]{0:T(256)} %param.11) | copy-start | bytes 3076
  122.9 31.1 %copy-start.1 = (bf16[1,4,2,49,256]{4,3,2,1,0:T(8,128)(2,1)S(1)}, bf16[1,4,2,49,256]{4,3,2,1,0:T(8,128)(2,1)}, u32[]{:S(2)}) copy-start(bf16[1,4,2,49,256]{4,3,2,1,0:T(8,128)(2,1)} %copy-done) | copy-start | bytes 602116
  149.8 94.3 %copy-start.4 = (bf16[1,8,2,49,256]{4,2,3,1,0:T(2,128)(2,1)S(1)}, bf16[1,8,2,49,256]{4,2,3,1,0:T(2,128)(2,1)}, u32[]{:S(2)}) copy-start(bf16[1,8,2,49,256]{4,2,3,1,0:T(2,128)(2,1)} %param.17) | copy-start | bytes 1204228
  152.6 89.1 %collective-permute-start.1 = (bf16[1,4,2,49,256]{4,3,2,1,0:T(8,128)(2,1)}, bf16[1,4,2,49,256]{4,3,2,1,0:T(8,128)(2,1)}, u32[]{:S(2)}, u32[]{:S(2)}) collective-permute-start(bf16[1,4,2,49,256]{4,3,2,1,0:T(8,128)(2,1)} %get-tuple-element.47), channel_id=1, source_target_pairs={{0,4},{4,8},{8,12},{12,16},{16,20},{20,24},{24,28},{28,32},{32,36}... | collective-permute-start | bytes 602120 | tf_op jit(solution)/shard_map/ppermute | solution.py:12
  162.8 81.3 %collective-permute-start.3 = (bf16[1,4,2,49,256]{4,3,2,1,0:T(8,128)(2,1)S(1)}, bf16[1,4,2,49,256]{4,3,2,1,0:T(8,128)(2,1)S(1)}, u32[]{:S(2)}, u32[]{:S(2)}) collective-permute-start(bf16[1,4,2,49,256]{4,3,2,1,0:T(8,128)(2,1)S(1)} %get-tuple-element.45), channel_id=1, source_target_pairs={{0,4},{4,8},{8,12},{12,16},{16,20},{20,24},{24,28},{28,32},{32,36}... | collective-permute-start | bytes 602120 | tf_op jit(solution)/shard_map/ppermute | solution.py:12
Sparse Core Ops, SparseCore 0:
  162.1 256.6 all-reduce.6
where the time goes:
time: 435 us; the launch traced here: 430 us
  waiting for transfers between devices  174 us (40%)
  blocking collectives  78.9 us (18%)
  local copies, waits for them, and re-layouts  73.8 us (17%)
  matrix products  53.9 us (12%)
  other arithmetic  21 us (5%)
  between operations  15.4 us (4%)
  starting transfers between devices  13 us (3%)
    psum x1, waiting for transfers between devices, per_device(): lax.psum((grad_gain, grad_nbias, grad_qkv_w, grad_qkv_b, grad_proj_w, gra...  174 us
    psum x1, blocking collectives, per_device(): lax.psum((grad_gain, grad_nbias, grad_qkv_w, grad_qkv_b, grad_proj_w, gra...  78.9 us
    reshape x2, local copies, waits for them, and re-layouts, branch(): project_qkv.reshape(time_windows, WT, windows, patch_len, 3, head_count,...  22.6 us
    dot_general x3, matrix products, branch(): jnp.einsum('nwhqk,nwhke->nwhqe', attn_probs.astype(jnp.float32), values_f)  18.7 us
    dot_general x2, matrix products, branch(): jnp.einsum('nwhqe,nwhke->nwhqk', queries, keys_f) * head_depth ** (-0.5)  18.3 us
    ppermute x4, starting transfers between devices, passed_along(): lax.ppermute(array, axis, [(i, (i + by) % devices) for i in range(devices)])  12.9 us
    reshape x2, local copies, waits for them, and re-layouts, branch(): project_qkv.transpose(4, 0, 2, 5, 1, 3, 6)  11.7 us
  transfers between devices with their start and end apart: 5, of which 1 were waited for; matrix products, arithmetic and copies ran while one was open for 5% of the time, Pallas kernels for 0%

commit v1 on v0

v1 whole, which is shorter than its diff:
```python
import functools
import math

import jax
import jax.numpy as jnp
from jax import lax
from jax.experimental import pallas as pl
from jax.experimental.pallas import tpu as pltpu
from jax.sharding import PartitionSpec as P

HEADS = 8
WT = 8
HALF = WT // 2
AXES = ("frame", "clip")
BIG = 2.0**100
EXT = 16
f32, bf16 = jnp.float32, jnp.bfloat16


def passed_along(array, axis, by):
    devices = lax.axis_size(axis)
    return lax.ppermute(array, axis, [(i, (i + by) % devices) for i in range(devices)])


def mm(a, b, ca=1, cb=0):
    return lax.dot_general(a, b, (((ca,), (cb,)), ((), ())), preferred_element_type=f32)


def block_kernel(
    frame_total, sc, tok, gr, halo, gain, nb, w, wT, wp, wpT, bq, bp,
    mixed, gtok, send, pay,
    xs, gs, normT, gN, qkvT, doT, attT, dqT, acc,
):
    frames, windows, patch, width = tok.shape
    rows = WT * patch
    depth = width // HEADS
    scale = depth ** (-0.5)
    length, first = sc[0], sc[1]

    def frame_of(u):
        t = first + u
        return jnp.where(t >= frame_total, t - frame_total, t)

    def valid_of(u):
        return jnp.where(frame_of(u) < length, 1.0, 0.0).astype(f32)

    for win in range(windows):
        for u in range(WT):
            at = pl.ds(u * patch, patch)
            x_u = tok[HALF + u, win] if u < HALF else halo[0, u - HALF, win]
            g_u = gr[HALF + u, win] if u < HALF else halo[1, u - HALF, win]
            xs[win, at, :] = x_u.astype(f32)
            gs[win, at, :] = g_u.astype(f32) * valid_of(u)

    lane = lax.broadcasted_iota(jnp.int32, (EXT, rows), 1)
    row = lax.broadcasted_iota(jnp.int32, (EXT, rows), 0)
    u_lane = jnp.zeros((EXT, rows), jnp.int32)
    for u in range(1, WT):
        u_lane = u_lane + jnp.where(lane >= u * patch, 1, 0)
    t_lane = frame_of(u_lane)
    bad = jnp.where(t_lane < length, 0.0, 1.0)
    reg = jnp.where(t_lane < HALF, 1.0, 0.0)
    q_ext = jnp.where(row == 0, 1.0, jnp.where(row == 1, reg, jnp.where(row == 2, 1.0 - reg, 0.0)))
    k_ext = jnp.where(row == 0, bad, jnp.where(row == 1, 1.0 - reg, jnp.where(row == 2, reg, 0.0)))
    q_ext = q_ext.astype(bf16)
    k_ext = (k_ext * -BIG).astype(bf16)
    one_row = jnp.where(row == 0, 1.0, 0.0).astype(bf16)
    two_rows = jnp.where(row < 2, 1.0, 0.0).astype(bf16)

    bqT = jnp.transpose(jnp.broadcast_to(bq[...], (rows, bq.shape[1])))
    for win in range(windows):
        x = xs[win]
        mean = jnp.mean(x, axis=-1, keepdims=True)
        xc = x - mean
        var = jnp.mean(xc * xc, axis=-1, keepdims=True)
        normed = xc * lax.rsqrt(var + 1e-05) * gain[...] + nb[...]
        normT[win, :width, :] = jnp.transpose(normed).astype(bf16)
        normT[win, width:, :] = one_row
        attT[win, width:, :] = one_row
        qkvT[win] = (mm(wT[...], normT[win, :width, :]) + bqT).astype(bf16)
        gN[win] = gs[win].astype(bf16)
        doT[win] = mm(wp[...], gN[win], 1, 1).astype(bf16)

    def head(i, carry):
        win = i // HEADS
        h = i % HEADS
        at = pl.ds(pl.multiple_of(h * depth, depth), depth)
        at_k = pl.ds(pl.multiple_of(width + h * depth, depth), depth)
        at_v = pl.ds(pl.multiple_of(2 * width + h * depth, depth), depth)
        qT = qkvT[win, at, :]
        kT = qkvT[win, at_k, :]
        vT = qkvT[win, at_v, :]
        d_oT = doT[win, at, :]
        sT = mm(jnp.concatenate([kT, k_ext], 0), jnp.concatenate([qT, q_ext], 0), 0, 0)
        top = jnp.max(sT, axis=0, keepdims=True)
        e = jnp.exp2((sT - top) * (scale * math.log2(math.e)))
        eb = e.astype(bf16)
        summed = mm(jnp.concatenate([vT, one_row], 0), eb)
        inv = 1.0 / summed[depth : depth + 1]
        oT = (summed[:depth] * inv).astype(bf16)
        attT[win, at, :] = oT
        d_o = d_oT.astype(f32)
        delta = jnp.sum(d_o * oT.astype(f32), axis=0, keepdims=True) * inv
        d_on = (d_o * inv).astype(bf16)
        hi = delta.astype(bf16).astype(f32)
        lo = delta - hi
        d_ext = jnp.where(row == 0, -hi, jnp.where(row == 1, -lo, 0.0)).astype(bf16)
        dpT = mm(jnp.concatenate([vT, two_rows], 0), jnp.concatenate([d_on, d_ext], 0), 0, 0)
        dsT = (e * dpT).astype(bf16)
        dqT[win, at_v, :] = mm(d_on, eb, 1, 1).astype(bf16)
        dqT[win, at, :] = (mm(kT, dsT) * scale).astype(bf16)
        dqT[win, at_k, :] = (mm(qT, dsT, 1, 1) * scale).astype(bf16)
        return carry

    lax.fori_loop(0, windows * HEADS, head, 0)

    for win in range(windows):
        wide = 3 * width
        dw = mm(normT[win], dqT[win], 1, 1)
        dp = mm(attT[win], gN[win])
        if win == 0:
            acc[: width + EXT, :wide] = dw
            acc[: width + EXT, wide:] = dp
        else:
            acc[: width + EXT, :wide] += dw
            acc[: width + EXT, wide:] += dp
        gs[win] = jnp.transpose(mm(wpT[...], attT[win, :width, :])) + bp[...]
        for u in range(WT):
            b_u = (gs[win, pl.ds(u * patch, patch), :] * valid_of(u)).astype(bf16)
            if u < HALF:
                x_u = tok[HALF + u, win].astype(f32)
                mixed[HALF + u, win] = (x_u + b_u.astype(f32)).astype(bf16)
            else:
                send[0, u - HALF, win] = b_u
        dn = jnp.transpose(mm(w[...], dqT[win]).astype(bf16).astype(f32))
        x = xs[win]
        mean = jnp.mean(x, axis=-1, keepdims=True)
        xc = x - mean
        rstd = lax.rsqrt(jnp.mean(xc * xc, axis=-1, keepdims=True) + 1e-05)
        xhat = xc * rstd
        dgain = jnp.sum(dn * xhat, axis=0, keepdims=True)
        dbias = jnp.sum(dn, axis=0, keepdims=True)
        if win == 0:
            acc[width + EXT : width + EXT + 1, :width] = dgain
            acc[width + EXT : width + EXT + 1, width : 2 * width] = dbias
        else:
            acc[width + EXT : width + EXT + 1, :width] += dgain
            acc[width + EXT : width + EXT + 1, width : 2 * width] += dbias
        dxh = dn * gain[...]
        m1 = jnp.mean(dxh, axis=-1, keepdims=True)
        m2 = jnp.mean(dxh * xhat, axis=-1, keepdims=True)
        xs[win] = rstd * (dxh - m1 - xhat * m2)
        for u in range(WT):
            d_u = xs[win, pl.ds(u * patch, patch), :].astype(bf16)
            if u < HALF:
                g_u = gr[HALF + u, win].astype(f32)
                gtok[HALF + u, win] = (g_u + d_u.astype(f32)).astype(bf16)
            else:
                send[1, u - HALF, win] = d_u
    acc[width + EXT : width + EXT + 1, 2 * width :] = jnp.zeros((1, 2 * width), f32)
    acc[width + EXT + 1 :, :] = jnp.zeros((EXT - 1, 4 * width), f32)
    chunks, deep, lanes = pay.shape
    across = 4 * width // lanes
    for c in range(chunks):
        r, k = c // across, c % across
        pay[c] = acc[r * deep : (r + 1) * deep, k * lanes : (k + 1) * lanes].astype(bf16)


def final_kernel(
    width, recv, tok, gr, got, mixed_in, gtok_in,
    mixed, gtok, dgain, dnb, dwq, dbq, dwp, dbp, full,
):
    mixed[...] = (tok[...].astype(f32) + recv[0].astype(f32)).astype(bf16)
    gtok[...] = (gr[...].astype(f32) + recv[1].astype(f32)).astype(bf16)
    chunks, deep, lanes = got.shape
    across = 4 * width // lanes
    for c in range(chunks):
        r, k = c // across, c % across
        full[r * deep : (r + 1) * deep, k * lanes : (k + 1) * lanes] = got[c].astype(f32)
    dwq[...] = full[:width, : 3 * width]
    dwp[...] = full[:width, 3 * width :]
    dbq[...] = full[width : width + 1, : 3 * width]
    dbp[...] = full[width : width + 1, 3 * width :]
    dgain[...] = full[width + EXT : width + EXT + 1, :width]
    dnb[...] = full[width + EXT : width + EXT + 1, width : 2 * width]


def groups_of(bits, devices):
    offsets = []
    for m in range(1 << len(bits)):
        offsets.append(sum(1 << b for k, b in enumerate(bits) if m >> k & 1))
    mask = sum(1 << b for b in bits)
    return [[base | o for o in offsets] for base in range(devices) if not base & mask]


def exchange(x, bits):
    devices = lax.axis_size(AXES)
    return lax.all_to_all(
        x, AXES, 0, 0, tiled=True, axis_index_groups=groups_of(bits, devices)
    )


NEAR = (0, 1, 5, 6, 7)
ALONG_Z = (2, 3, 4)


def per_device(
    tokens, lengths, norm_gain, norm_bias, qkv_weight, qkv_bias, proj_weight, proj_bias, grad_out
):
    _, frames, windows, patch, width = tokens.shape
    rows = WT * patch
    frame_total = frames * lax.axis_size("frame")
    first = lax.axis_index("frame") * frames + HALF
    tok, gr = tokens[0], grad_out[0]
    halo = passed_along(jnp.stack([tok[:HALF], gr[:HALF]]), "frame", -1)
    w = qkv_weight.astype(bf16)
    wp = proj_weight.astype(bf16)
    sc = jnp.stack([lengths[0], first]).astype(jnp.int32)
    vmem = pl.BlockSpec(memory_space=pltpu.VMEM)
    near = 1 << len(NEAR)
    deep = (width + 2 * EXT) * 4 * width // 128 // near
    half = (HALF, windows, patch, width)
    slab = jax.ShapeDtypeStruct(tok.shape, bf16)
    mixed, gtok, send, pay = pl.pallas_call(
        functools.partial(block_kernel, frame_total),
        name="block",
        out_shape=(
            slab,
            slab,
            jax.ShapeDtypeStruct((2,) + half, bf16),
            jax.ShapeDtypeStruct((near, deep, 128), bf16),
        ),
        in_specs=[pl.BlockSpec(memory_space=pltpu.SMEM)] + [vmem] * 11,
        out_specs=(vmem,) * 4,
        scratch_shapes=[
            pltpu.VMEM((windows, rows, width), f32),
            pltpu.VMEM((windows, rows, width), f32),
            pltpu.VMEM((windows, width + EXT, rows), bf16),
            pltpu.VMEM((windows, rows, width), bf16),
            pltpu.VMEM((windows, 3 * width, rows), bf16),
            pltpu.VMEM((windows, width, rows), bf16),
            pltpu.VMEM((windows, width + EXT, rows), bf16),
            pltpu.VMEM((windows, 3 * width, rows), bf16),
            pltpu.VMEM((width + 2 * EXT, 4 * width), f32),
        ],
        compiler_params=pltpu.CompilerParams(vmem_limit_bytes=48 << 20),
    )(
        sc, tok, gr, halo, norm_gain[None], norm_bias[None], w, w.T, wp, wp.T,
        qkv_bias[None], proj_bias[None],
    )
    recv = passed_along(send, "frame", 1)
    part = jnp.sum(exchange(pay, NEAR).astype(f32), axis=0)
    deeper = 1 << len(ALONG_Z)
    total = jnp.sum(exchange(jnp.broadcast_to(part, (deeper,) + part.shape), ALONG_Z), axis=0)
    got = exchange(jnp.broadcast_to(total.astype(bf16), (near,) + part.shape), NEAR)

    def whole(*shape):
        return pl.BlockSpec(shape, lambda i: (0,) * len(shape))

    anywhere = pl.BlockSpec(memory_space=pl.ANY)
    mixed, gtok, dgain, dnb, dwq, dbq, dwp, dbp = pl.pallas_call(
        functools.partial(final_kernel, width),
        name="final",
        grid=(1,),
        out_shape=(
            slab,
            slab,
            jax.ShapeDtypeStruct((1, width), f32),
            jax.ShapeDtypeStruct((1, width), f32),
            jax.ShapeDtypeStruct((width, 3 * width), f32),
            jax.ShapeDtypeStruct((1, 3 * width), f32),
            jax.ShapeDtypeStruct((width, width), f32),
            jax.ShapeDtypeStruct((1, width), f32),
        ),
        in_specs=[
            whole(2, *half), whole(*half), whole(*half), whole(near, deep, 128),
            anywhere, anywhere,
        ],
        out_specs=(
            whole(*half), whole(*half), whole(1, width), whole(1, width),
            whole(width, 3 * width), whole(1, 3 * width), whole(width, width), whole(1, width),
        ),
        scratch_shapes=[pltpu.VMEM((width + 2 * EXT, 4 * width), f32)],
        input_output_aliases={4: 0, 5: 1},
        compiler_params=pltpu.CompilerParams(vmem_limit_bytes=32 << 20),
    )(recv, tok, gr, got, mixed, gtok)
    return (mixed[None], gtok[None], dgain[0], dnb[0], dwq, dbq[0], dwp, dbp[0])


def solution(mesh):
    split = P("clip", "frame", None, None, None)
    in_specs = (split, P("clip"), P(), P(), P(), P(), P(), P(), split)
    out_specs = (split, split, P(), P(), P(), P(), P(), P())
    return jax.shard_map(
        per_device, mesh=mesh, in_specs=in_specs, out_specs=out_specs, check_vma=False
    )
```

time: 435 us -> 113 us (0.26); the launches traced: 430 us -> 113 us
  waiting for transfers between devices: 174 us -> 29.4 us
  local copies, waits for them, and re-layouts: 73.8 us -> 5.59 us
  matrix products: 53.9 us -> 0 us
  blocking collectives: 78.9 us -> 35.8 us
  Pallas kernels: 0 us -> 21.8 us
  other arithmetic: 21 us -> 1.61 us
  between operations: 15.4 us -> 1.49 us
  starting transfers between devices: 13 us -> 17.6 us
    psum x1 -> x0, waiting for transfers between devices: 174 us -> none  [per_device(): lax.psum((grad_gain, grad_nbias, grad_qkv_w, grad_qkv_b, grad_proj_w, gra...]
    psum x1 -> x0, blocking collectives: 78.9 us -> none  [per_device(): lax.psum((grad_gain, grad_nbias, grad_qkv_w, grad_qkv_b, grad_proj_w, gra...]
    dot_general x11 -> x0, matrix products: 45.5 us -> none  [the longest x3 18.7 us: branch(): jnp.einsum('nwhqk,nwhke->nwhqe', attn_probs.astype(jnp.float32), values_f)]
    reshape x9 -> x0, local copies, waits for them, and re-layouts: 44.9 us -> none  [the longest x2 22.6 us: branch(): project_qkv.reshape(time_windows, WT, windows, patch_len, 3, head_count,...]
    all_to_all x0 -> x2, blocking collectives: none -> 35.8 us  [exchange(): lax.all_to_all(x, AXES, 0, 0, tiled=True, axis_index_groups=groups_of(bit...]
    ppermute x4 -> x2, waiting for transfers between devices: 0.01 us -> 24.9 us  [passed_along(): lax.ppermute(array, axis, [(i, (i + by) % devices) for i in range(devices)])]
    pallas_call x0 -> x2, Pallas kernels: none -> 21.8 us  [the longest x1 20.6 us: per_device(): pl.pallas_call(functools.partial(block_kernel, frame_total), name='block'...]
    reduce_sum x6 -> x2, other arithmetic: 12.8 us -> 0.11 us  [the longest x1 0.09 us: per_device(): part = jnp.sum(exchange(pay, NEAR).astype(f32), axis=0)]
  transfers between devices with their start and end apart: 5 -> 3, of which waited for: 1 -> 3; matrix products, arithmetic and copies ran while one was open for 5% -> 1% of each run, Pallas kernels for 0% -> 0%
where the time goes in v1:
time: 113 us
  blocking collectives  35.8 us (32%)
  waiting for transfers between devices  29.4 us (26%)
  Pallas kernels  21.8 us (19%)
  starting transfers between devices  17.6 us (16%)
  local copies, waits for them, and re-layouts  5.59 us (5%)
  other arithmetic  1.61 us (1%)
  between operations  1.49 us (1%)
    all_to_all x2, blocking collectives, exchange(): lax.all_to_all(x, AXES, 0, 0, tiled=True, axis_index_groups=groups_of(bit...  35.8 us
    ppermute x2, waiting for transfers between devices, passed_along(): lax.ppermute(array, axis, [(i, (i + by) % devices) for i in range(devices)])  24.9 us
    pallas_call x1, Pallas kernels, per_device(): pl.pallas_call(functools.partial(block_kernel, frame_total), name='block'...  20.6 us
    ppermute x2, starting transfers between devices, passed_along(): lax.ppermute(array, axis, [(i, (i + by) % devices) for i in range(devices)])  11.7 us
    all_to_all x1, starting transfers between devices, exchange(): lax.all_to_all(x, AXES, 0, 0, tiled=True, axis_index_groups=groups_of(bit...  5.88 us
    all_to_all x1, waiting for transfers between devices, exchange(): lax.all_to_all(x, AXES, 0, 0, tiled=True, axis_index_groups=groups_of(bit...  4.44 us
    unnamed x26, local copies, waits for them, and re-layouts  3.15 us
  transfers between devices with their start and end apart: 3, of which 3 were waited for; matrix products, arithmetic and copies ran while one was open for 1% of the time, Pallas kernels for 0%

profile of v1, /device:TPU:1, one launch (start us, length us, event | category | flops | bytes accessed | tf_op | source)
XLA Modules:
  0.0 113.1 jit_solution(9228477532217752100)
XLA Ops:
  0.6 0.0 slice-start
  0.6 1.1 slice.10
  1.8 0.0 copy-start.9
  1.8 0.0 copy-start.8
  1.8 0.0 slice-done
  1.9 0.0 copy-start.7
  1.9 0.8 pad_maximum_fusion
  2.7 11.3 %collective-permute-start = (bf16[2,4,2,49,256]{4,3,2,1,0:T(8,128)(2,1)}, bf16[2,4,2,49,256]{4,3,2,1,0:T(8,128)(2,1)S(1)}, u32[]{:S(2)}, u32[]{:S(2)}) collective-permute-start(bf16[2,4,2,49,256]{4,3,2,1,0:T(8,128)(2,1)} %pad_maximum_fusion), channel_id=1, source_target_pairs={{0,252},{4,0},{8,4},{12,8},{16,12},{20,16},{24,20},{28,24},{32,28}... | collective-permute-start | bytes 1204232 | tf_op jit(solution)/shard_map/ppermute | solution.py:22
  14.7 0.0 copy-done.9
  14.7 0.0 copy-done.8
  14.7 0.1 copy.34
  14.8 0.1 copy.36.wp
  14.9 0.0 copy-done.7
  14.9 0.0 copy-start.5
  14.9 0.0 copy-start.6
  14.9 0.2 copy.33
  15.1 0.2 copy.35.w
  15.3 0.1 pad_add_fusion.sc
  15.4 0.5 copy-done.5
  15.9 0.1 copy-done.6
  16.0 0.0 copy-start
  16.0 0.0 copy-start.1
  16.0 0.0 copy-start.2
  16.0 0.1 copy_bitcast_fusion
  16.2 7.3 %collective-permute-done.halo = bf16[2,4,2,49,256]{4,3,2,1,0:T(8,128)(2,1)S(1)} collective-permute-done((bf16[2,4,2,49,256]{4,3,2,1,0:T(8,128)(2,1)}, bf16[2,4,2,49,256]{4,3,2,1,0:T(8,128)(2,1)S(1)}, u32[]{:S(2)}, u32[]{:S(2)}) %collective-permute-start) | collective-permute-done | bytes 401440 | tf_op jit(solution)/shard_map/ppermute | solution.py:22
  23.5 0.0 copy-done
  23.5 0.0 copy-done.1
  23.5 0.0 copy-done.2
  23.5 20.6 %block.1 = (bf16[8,2,49,256]{3,2,1,0:T(8,128)(2,1)S(1)}, bf16[8,2,49,256]{3,2,1,0:T(8,128)(2,1)S(1)}, bf16[2,4,2,49,256]{4,3,2,1,0:T(8,128)(2,1)S(1)}, bf16[32,72,128]{2,1,0:T(8,128)(2,1)S(1)}) custom-call(s32[2]{0:T(128)S(1)} %pad_add_fusion.sc, bf16[8,2,49,256]{3,2,1,0:T(8,128)(2,1)S(1)} %get-tuple-element.49.tok, ...), custom_call_target="tpu_custom_call" | custom-call | tf_op jit(solution)/shard_map/block/pallas_call | solution.py:224
  44.1 0.0 copy-start.3
  44.1 16.5 %all_to_all.15 = bf16[32,72,128]{2,1,0:T(8,128)(2,1)S(1)} all-to-all(bf16[32,72,128]{2,1,0:T(8,128)(2,1)S(1)} %get-tuple-element.21), channel_id=1, replica_groups={{0,1,2,3,32,33,34,35,64,65,66,67,96,97,98,99,128,129,130,131,160,161,16..., dimensions={0} | all-to-all | bytes 1179648 | tf_op jit(solution)/shard_map/all_to_all | solution.py:198
  60.6 0.1 convert_reduce_fusion
  60.7 0.0 copy-done.3
  60.7 19.3 %all_to_all.16 = f32[8,72,128]{2,1,0:T(8,128)S(1)} all-to-all(f32[8,72,128]{2,1,0:T(8,128)S(1)} %broadcast_in_dim.28), channel_id=1, replica_groups={{0,4,8,12,16,20,24,28},{1,5,9,13,17,21,25,29},{2,6,10,14,18,22,26,30},{..., dimensions={0} | all-to-all | bytes 589824 | tf_op jit(solution)/shard_map/all_to_all | solution.py:198
  80.0 0.0 copy-start.4
  80.0 0.9 broadcast_in_dim.29
  80.9 5.9 %all-to-all-start.2 = ((bf16[32,72,128]{2,1,0:T(8,128)(2,1)}), bf16[32,72,128]{2,1,0:T(8,128)(2,1)S(1)}, u32[]{:S(2)}, u32[]{:S(2)}) async-start(bf16[32,72,128]{2,1,0:T(8,128)(2,1)} %broadcast_in_dim.29), calls=%async_computation.2 | async-start | bytes 1179648 | tf_op jit(solution)/shard_map/all_to_all | solution.py:198
  86.8 0.0 copy-done.4
  86.8 0.4 collective-permute-start.1
  87.2 17.6 %collective-permute-done.1.recv = bf16[2,4,2,49,256]{4,3,2,1,0:T(8,128)(2,1)S(1)} collective-permute-done((bf16[2,4,2,49,256]{4,3,2,1,0:T(8,128)(2,1)S(1)}, bf16[2,4,2,49,256]{4,3,2,1,0:T(8,128)(2,1)S(1)}, u32[]{:S(2)}, u32[]{:S(2)}) %collective-permute-start.1) | collective-permute-done | bytes 401440 | tf_op jit(solution)/shard_map/ppermute | solution.py:22
  104.8 4.4 %all-to-all-done.2.got = bf16[32,72,128]{2,1,0:T(8,128)(2,1)S(1)} async-done(((bf16[32,72,128]{2,1,0:T(8,128)(2,1)}), bf16[32,72,128]{2,1,0:T(8,128)(2,1)S(1)}, u32[]{:S(2)}, u32[]{:S(2)}) %all-to-all-start.2) | async-done | bytes 589856 | tf_op jit(solution)/shard_map/all_to_all | solution.py:198
  109.2 1.2 %final.1 = (bf16[8,2,49,256]{3,2,1,0:T(8,128)(2,1)S(1)}, bf16[8,2,49,256]{3,2,1,0:T(8,128)(2,1)S(1)}, f32[1,256]{1,0:T(1,128)}, f32[1,256]{1,0:T(1,128)}, f32[25...) custom-call(bf16[2,4,2,49,256]{4,3,2,1,0:T(8,128)(2,1)S(1)} %collect, ...), custom_call_target="tpu_custom_call", output_to_operand_aliasing={{0}: (4, {}), {1}: (5, {})} | custom-call | tf_op jit(solution)/shard_map/final/pallas_call | solution.py:261
  110.4 1.1 copy.37
  111.5 1.1 copy.38
  112.5 0.6 reduce
  (5 shorter events, 0.1 us)
Async XLA Ops:
  0.6 1.2 %slice-start = ((bf16[1,8,2,49,256]{4,2,3,1,0:T(2,128)(2,1)}), bf16[1,4,2,49,256]{4,2,3,1,0:T(2,128)(2,1)S(1)}, s32[]{:S(2)}) async-start(bf16[1,8,2,49,256]{4,2,3,1,0:T(2,128)(2,1)} %param.17), calls=%async_computation.3 | async-start | bytes 401408 | tf_op jit(solution)/shard_map/slice | solution.py:215
  1.8 12.9 %copy-start.9 = (f32[768]{0:T(1024)S(1)}, f32[768]{0:T(1024)}, u32[]{:S(2)}) copy-start(f32[768]{0:T(1024)} %param.14) | copy-start | bytes 9220
  1.8 12.9 %copy-start.8 = (f32[256,256]{1,0:T(8,128)S(1)}, f32[256,256]{1,0:T(8,128)}, u32[]{:S(2)}) copy-start(f32[256,256]{1,0:T(8,128)} %param.15) | copy-start | bytes 786436
  1.9 13.0 %copy-start.7 = (f32[256,768]{1,0:T(8,128)S(1)}, f32[256,768]{1,0:T(8,128)}, u32[]{:S(2)}) copy-start(f32[256,768]{1,0:T(8,128)} %param.13) | copy-start | bytes 2359300
  2.7 20.8 %collective-permute-start = (bf16[2,4,2,49,256]{4,3,2,1,0:T(8,128)(2,1)}, bf16[2,4,2,49,256]{4,3,2,1,0:T(8,128)(2,1)S(1)}, u32[]{:S(2)}, u32[]{:S(2)}) collective-permute-start(bf16[2,4,2,49,256]{4,3,2,1,0:T(8,128)(2,1)} %pad_maximum_fusion), channel_id=1, source_target_pairs={{0,252},{4,0},{8,4},{12,8},{16,12},{20,16},{24,20},{28,24},{32,28}... | collective-permute-start | bytes 1204232 | tf_op jit(solution)/shard_map/ppermute | solution.py:22
  14.9 1.0 copy-start.5
  14.9 1.1 copy-start.6
  16.0 7.5 %copy-start = (f32[256]{0:T(256)S(1)}, f32[256]{0:T(256)}, u32[]{:S(2)}) copy-start(f32[256]{0:T(256)} %param.11) | copy-start | bytes 3076
  16.0 7.5 %copy-start.1 = (f32[256]{0:T(256)S(1)}, f32[256]{0:T(256)}, u32[]{:S(2)}) copy-start(f32[256]{0:T(256)} %param.12) | copy-start | bytes 3076
  16.0 7.5 %copy-start.2 = (f32[256]{0:T(256)S(1)}, f32[256]{0:T(256)}, u32[]{:S(2)}) copy-start(f32[256]{0:T(256)} %param.16) | copy-start | bytes 3076
  44.1 16.6 %copy-start.3 = (bf16[2,4,2,49,256]{4,3,2,1,0:T(8,128)(2,1)}, bf16[2,4,2,49,256]{4,3,2,1,0:T(8,128)(2,1)S(1)}, u32[]{:S(2)}) copy-start(bf16[2,4,2,49,256]{4,3,2,1,0:T(8,128)(2,1)S(1)} %get-tuple-element.20) | copy-start | bytes 1204228
  80.0 6.8 %copy-start.4 = (bf16[2,4,2,49,256]{4,3,2,1,0:T(8,128)(2,1)S(1)}, bf16[2,4,2,49,256]{4,3,2,1,0:T(8,128)(2,1)}, u32[]{:S(2)}) copy-start(bf16[2,4,2,49,256]{4,3,2,1,0:T(8,128)(2,1)} %copy-done.3) | copy-start | bytes 1204228
  80.9 28.3 %all-to-all-start.2 = ((bf16[32,72,128]{2,1,0:T(8,128)(2,1)}), bf16[32,72,128]{2,1,0:T(8,128)(2,1)S(1)}, u32[]{:S(2)}, u32[]{:S(2)}) async-start(bf16[32,72,128]{2,1,0:T(8,128)(2,1)} %broadcast_in_dim.29), calls=%async_computation.2 | async-start | bytes 1179648 | tf_op jit(solution)/shard_map/all_to_all | solution.py:198
  86.8 18.0 %collective-permute-start.1 = (bf16[2,4,2,49,256]{4,3,2,1,0:T(8,128)(2,1)S(1)}, bf16[2,4,2,49,256]{4,3,2,1,0:T(8,128)(2,1)S(1)}, u32[]{:S(2)}, u32[]{:S(2)}) collective-permute-start(bf16[2,4,2,49,256]{4,3,2,1,0:T(8,128)(2,1)S(1)} %copy-done.4), channel_id=1, source_target_pairs={{0,4},{4,8},{8,12},{12,16},{16,20},{20,24},{24,28},{28,32},{32,36}... | collective-permute-start | bytes 1204232 | tf_op jit(solution)/shard_map/ppermute | solution.py:22

commit v2 on v1

v2 whole, which is shorter than its diff:
```python
import functools
import math

import jax
import jax.numpy as jnp
from jax import lax
from jax.experimental import pallas as pl
from jax.experimental.pallas import tpu as pltpu
from jax.sharding import PartitionSpec as P

HEADS = 8
WT = 8
HALF = WT // 2
AXES = ("frame", "clip")
BIG = 2.0**100
UNROLL = 2
EXT = 16
f32, bf16 = jnp.float32, jnp.bfloat16


def swapped(array, odd):
    devices = lax.axis_size("frame")
    pairs = [(i, (((i + odd) ^ 1) - odd) % devices) for i in range(devices)]
    return lax.ppermute(array, "frame", pairs)


def mm(a, b, ca=1, cb=0):
    return lax.dot_general(a, b, (((ca,), (cb,)), ((), ())), preferred_element_type=f32)


def role(place, odd, frames):
    first = lax.rem(place, 2) == odd
    own_start = jnp.where(first, HALF, 0)
    win = jnp.where(first, 0, 1)
    return first, own_start, win


def pick_kernel(tok, gr, out):
    _, start, win = role(lax.axis_index("frame"), 1, tok.shape[0])
    for k in range(HALF):
        out[0, k] = tok[start + k, 1 - win]
        out[1, k] = gr[start + k, 1 - win]


def block_kernel(
    frame_total, last, lengths, tok, gr, halo, gain, nb, w, wT, wp, wpT, bq, bp, *refs
):
    if last:
        acc_in, mixed, gtok, send, pay = refs[:5]
    else:
        mixed, gtok, send, acc_out = refs[:4]
    xs, gs, normT, gN, qkvT, doT, attT, dqT, acc, ext = refs[-10:]
    patch, width = tok.shape[2:]
    rows = WT * patch
    depth = width // HEADS
    scale = depth ** (-0.5)
    length = lengths[0]
    frames = tok.shape[0]
    place = lax.axis_index("frame")
    first, own_start, win = role(place, int(last), frames)
    own_frame = place * frames + own_start
    halo_frame = place * frames + jnp.where(first, frames, -HALF)
    halo_frame = jnp.where(halo_frame < 0, halo_frame + frame_total, halo_frame)
    halo_frame = jnp.where(halo_frame >= frame_total, halo_frame - frame_total, halo_frame)

    def valid_of(u):
        t = own_frame + u if u < HALF else halo_frame + (u - HALF)
        return jnp.where(t < length, 1.0, 0.0).astype(f32)

    for u in range(WT):
        at = pl.ds(u * patch, patch)
        k = u % HALF
        if u < HALF:
            x_u, g_u = tok[own_start + k, win], gr[own_start + k, win]
        else:
            x_u, g_u = halo[0, k], halo[1, k]
        xs[at, :] = x_u.astype(f32)
        gs[at, :] = g_u.astype(f32) * valid_of(u)

    lane = lax.broadcasted_iota(jnp.int32, (EXT, rows), 1)
    row = lax.broadcasted_iota(jnp.int32, (EXT, rows), 0)
    u_lane = jnp.zeros((EXT, rows), jnp.int32)
    for u in range(1, WT):
        u_lane = u_lane + jnp.where(lane >= u * patch, 1, 0)
    t_lane = jnp.where(u_lane < HALF, own_frame + u_lane, halo_frame + u_lane - HALF)
    bad = jnp.where(t_lane < length, 0.0, 1.0)
    reg = jnp.where(t_lane < HALF, 1.0, 0.0)
    q_rows = jnp.where(row == 1, reg, jnp.where(row == 2, 1.0 - reg, 0.0))
    k_rows = jnp.where(row == 1, 1.0 - reg, jnp.where(row == 2, reg, 0.0))
    ext[0] = jnp.where(row == 0, 1.0, q_rows).astype(bf16)
    ext[1] = (jnp.where(row == 0, bad, k_rows) * -BIG).astype(bf16)
    one_row = jnp.where(row == 0, 1.0, 0.0).astype(bf16)
    two_rows = jnp.where(row < 2, 1.0, 0.0).astype(bf16)

    bqT = jnp.transpose(jnp.broadcast_to(bq[...], (rows, bq.shape[1])))
    x = xs[...]
    mean = jnp.mean(x, axis=-1, keepdims=True)
    xc = x - mean
    var = jnp.mean(xc * xc, axis=-1, keepdims=True)
    rstd = lax.rsqrt(var + 1e-05)
    xhat = xc * rstd
    xs[...] = xhat
    normed = xhat * gain[...] + nb[...]
    normT[:width, :] = jnp.transpose(normed).astype(bf16)
    normT[width:, :] = one_row
    attT[width:, :] = one_row
    qkvT[...] = (mm(wT[...], normT[:width, :]) + bqT).astype(bf16)
    gN[...] = gs[...].astype(bf16)
    doT[...] = mm(wp[...], gN[...], 1, 1).astype(bf16)

    def head(h):
        at = pl.ds(pl.multiple_of(h * depth, depth), depth)
        at_k = pl.ds(pl.multiple_of(width + h * depth, depth), depth)
        at_v = pl.ds(pl.multiple_of(2 * width + h * depth, depth), depth)
        qT = qkvT[at, :]
        kT = qkvT[at_k, :]
        vT = qkvT[at_v, :]
        d_oT = doT[at, :]
        sT = mm(jnp.concatenate([kT, ext[1]], 0), jnp.concatenate([qT, ext[0]], 0), 0, 0)
        top = jnp.max(sT, axis=0, keepdims=True)
        e = jnp.exp2((sT - top) * (scale * math.log2(math.e)))
        eb = e.astype(bf16)
        summed = mm(jnp.concatenate([vT, one_row], 0), eb)
        inv = 1.0 / summed[depth : depth + 1]
        oT = (summed[:depth] * inv).astype(bf16)
        attT[at, :] = oT
        d_o = d_oT.astype(f32)
        delta = jnp.sum(d_o * oT.astype(f32), axis=0, keepdims=True) * inv
        d_on = (d_o * inv).astype(bf16)
        hi = delta.astype(bf16).astype(f32)
        lo = delta - hi
        d_ext = jnp.where(row == 0, -hi, jnp.where(row == 1, -lo, 0.0)).astype(bf16)
        dpT = mm(jnp.concatenate([vT, two_rows], 0), jnp.concatenate([d_on, d_ext], 0), 0, 0)
        dsT = (e * dpT).astype(bf16)
        dqT[at_v, :] = mm(d_on, eb, 1, 1).astype(bf16)
        dqT[at, :] = (mm(kT, dsT) * scale).astype(bf16)
        dqT[at_k, :] = (mm(qT, dsT, 1, 1) * scale).astype(bf16)

    def heads(i, carry):
        for k in range(UNROLL):
            head(i * UNROLL + k)
        return carry

    lax.fori_loop(0, HEADS // UNROLL, heads, 0)

    wide = 3 * width
    acc[: width + EXT, :wide] = mm(normT[...], dqT[...], 1, 1)
    acc[: width + EXT, wide:] = mm(attT[...], gN[...])
    gs[...] = jnp.transpose(mm(wpT[...], attT[:width, :])) + bp[...]
    for u in range(WT):
        k = u % HALF
        b_u = (gs[pl.ds(u * patch, patch), :] * valid_of(u)).astype(bf16)
        if u < HALF:
            x_u = tok[own_start + k, win].astype(f32)
            mixed[k] = (x_u + b_u.astype(f32)).astype(bf16)
        else:
            send[0, k] = b_u
    dn = jnp.transpose(mm(w[...], dqT[...]).astype(bf16).astype(f32))
    xhat = xs[...]
    small = width + EXT
    acc[small : small + 1, :width] = jnp.sum(dn * xhat, axis=0, keepdims=True)
    acc[small : small + 1, width : 2 * width] = jnp.sum(dn, axis=0, keepdims=True)
    acc[small : small + 1, 2 * width :] = jnp.zeros((1, 2 * width), f32)
    acc[small + 1 :, :] = jnp.zeros((EXT - 1, 4 * width), f32)
    dxh = dn * gain[...]
    m1 = jnp.mean(dxh, axis=-1, keepdims=True)
    m2 = jnp.mean(dxh * xhat, axis=-1, keepdims=True)
    gs[...] = rstd * (dxh - m1 - xhat * m2)
    for u in range(WT):
        k = u % HALF
        d_u = gs[pl.ds(u * patch, patch), :].astype(bf16)
        if u < HALF:
            g_u = gr[own_start + k, win].astype(f32)
            gtok[k] = (g_u + d_u.astype(f32)).astype(bf16)
        else:
            send[1, k] = d_u
    if not last:
        acc_out[...] = acc[...]
    else:
        chunks, deep, lanes = pay.shape
        across = 4 * width // lanes
        for c in range(chunks):
            r, k = c // across, c % across
            at = (slice(r * deep, (r + 1) * deep), slice(k * lanes, (k + 1) * lanes))
            pay[c] = (acc_in[at] + acc[at]).astype(bf16)


def join_kernel(tok, gr, mixed1, gtok1, back1, mixed2, gtok2, back2, mixed, gtok):
    for n, (m, g, back) in enumerate(((mixed1, gtok1, back1), (mixed2, gtok2, back2))):
        _, start, win = role(lax.axis_index("frame"), n, tok.shape[0])
        other, other_win = start, 1 - win
        for k in range(HALF):
            mixed[start + k, win] = m[k]
            gtok[start + k, win] = g[k]
            at = other + k
            mixed[at, other_win] = (
                tok[at, other_win].astype(f32) + back[0, k].astype(f32)
            ).astype(bf16)
            gtok[at, other_win] = (
                gr[at, other_win].astype(f32) + back[1, k].astype(f32)
            ).astype(bf16)


def unpack_kernel(width, got, dgain, dnb, dwq, dbq, dwp, dbp, full):
    chunks, deep, lanes = got.shape
    across = 4 * width // lanes
    for c in range(chunks):
        r, k = c // across, c % across
        full[r * deep : (r + 1) * deep, k * lanes : (k + 1) * lanes] = got[c].astype(f32)
    dwq[...] = full[:width, : 3 * width]
    dwp[...] = full[:width, 3 * width :]
    dbq[...] = full[width : width + 1, : 3 * width]
    dbp[...] = full[width : width + 1, 3 * width :]
    dgain[...] = full[width + EXT : width + EXT + 1, :width]
    dnb[...] = full[width + EXT : width + EXT + 1, width : 2 * width]


def groups_of(bits, devices):
    offsets = []
    for m in range(1 << len(bits)):
        offsets.append(sum(1 << b for k, b in enumerate(bits) if m >> k & 1))
    mask = sum(1 << b for b in bits)
    return [[base | o for o in offsets] for base in range(devices) if not base & mask]


def exchange(x, bits):
    devices = lax.axis_size(AXES)
    return lax.all_to_all(
        x, AXES, 0, 0, tiled=True, axis_index_groups=groups_of(bits, devices)
    )


NEAR = (0, 1, 5, 6, 7)
ALONG_Z = (2, 3, 4)


def per_device(
    tokens, lengths, norm_gain, norm_bias, qkv_weight, qkv_bias, proj_weight, proj_bias, grad_out
):
    _, frames, windows, patch, width = tokens.shape
    rows = WT * patch
    frame_total = frames * lax.axis_size("frame")
    place = lax.axis_index("frame")
    tok, gr = tokens[0], grad_out[0]
    vmem = pl.BlockSpec(memory_space=pltpu.VMEM)
    smem = pl.BlockSpec(memory_space=pltpu.SMEM)
    half = jax.ShapeDtypeStruct((HALF, patch, width), bf16)
    halves = jax.ShapeDtypeStruct((2, HALF, patch, width), bf16)

    _, own_start, win = role(place, 0, frames)
    size = (1, HALF, 1, patch, width)
    at = (0, own_start, 1 - win, 0, 0)
    give1 = jnp.concatenate(
        [lax.dynamic_slice(a, at, size)[0, :, 0][None] for a in (tokens, grad_out)]
    )
    halo1 = swapped(give1, 0)
    give2 = pl.pallas_call(
        pick_kernel,
        name="pick",
        out_shape=halves,
        in_specs=[vmem] * 2,
        out_specs=vmem,
        compiler_params=pltpu.CompilerParams(vmem_limit_bytes=8 << 20),
    )(tok, gr)
    halo2 = swapped(give2, 1)
    w = qkv_weight.astype(bf16)
    wp = proj_weight.astype(bf16)
    near = 1 << len(NEAR)
    deep = (width + 2 * EXT) * 4 * width // 128 // near
    total_rows = width + 2 * EXT
    sums_type = jax.ShapeDtypeStruct((total_rows, 4 * width), f32)
    pay_type = jax.ShapeDtypeStruct((near, deep, 128), bf16)

    def block(last, halo, *more):
        return pl.pallas_call(
            functools.partial(block_kernel, frame_total, last),
            name="second_window" if last else "first_window",
            out_shape=(half, half, halves, pay_type if last else sums_type),
            in_specs=[smem] + [vmem] * (11 + len(more)),
            out_specs=(vmem,) * 4,
            scratch_shapes=[
                pltpu.VMEM((rows, width), f32),
                pltpu.VMEM((rows, width), f32),
                pltpu.VMEM((width + EXT, rows), bf16),
                pltpu.VMEM((rows, width), bf16),
                pltpu.VMEM((3 * width, rows), bf16),
                pltpu.VMEM((width, rows), bf16),
                pltpu.VMEM((width + EXT, rows), bf16),
                pltpu.VMEM((3 * width, rows), bf16),
                pltpu.VMEM((total_rows, 4 * width), f32),
                pltpu.VMEM((2, EXT, rows), bf16),
            ],
            compiler_params=pltpu.CompilerParams(vmem_limit_bytes=32 << 20),
            cost_estimate=pl.CostEstimate(
                flops=8_000_000_000, bytes_accessed=8_000_000, transcendentals=2_000_000
            ),
        )(
            lengths, tok, gr, halo, norm_gain[None], norm_bias[None], w, w.T, wp, wp.T,
            qkv_bias[None], proj_bias[None], *more,
        )

    mixed1, gtok1, send1, sums1 = block(False, halo1)
    back1 = swapped(send1, 0)
    mixed2, gtok2, send2, pay = block(True, halo2, sums1)
    pay, back1 = lax.optimization_barrier((pay, back1))
    part = jnp.sum(exchange(pay, NEAR).astype(f32), axis=0).astype(bf16)
    deeper = 1 << len(ALONG_Z)
    sums = exchange(jnp.broadcast_to(part, (deeper,) + part.shape), ALONG_Z)
    total = jnp.sum(sums.astype(f32), axis=0).astype(bf16)
    back2 = swapped(send2, 1)
    got = exchange(jnp.broadcast_to(total, (near,) + part.shape), NEAR)
    slab = jax.ShapeDtypeStruct(tok.shape, bf16)
    mixed, gtok = pl.pallas_call(
        join_kernel,
        name="join",
        out_shape=(slab, slab),
        in_specs=[vmem] * 8,
        out_specs=(vmem,) * 2,
        compiler_params=pltpu.CompilerParams(vmem_limit_bytes=16 << 20),
        cost_estimate=pl.CostEstimate(
            flops=20_000_000_000, bytes_accessed=4_000_000, transcendentals=0
        ),
    )(
        tok, gr,
        mixed1, gtok1, back1, mixed2, gtok2, back2,
    )
    dgain, dnb, dwq, dbq, dwp, dbp = pl.pallas_call(
        functools.partial(unpack_kernel, width),
        name="unpack",
        out_shape=(
            jax.ShapeDtypeStruct((1, width), f32),
            jax.ShapeDtypeStruct((1, width), f32),
            jax.ShapeDtypeStruct((width, 3 * width), f32),
            jax.ShapeDtypeStruct((1, 3 * width), f32),
            jax.ShapeDtypeStruct((width, width), f32),
            jax.ShapeDtypeStruct((1, width), f32),
        ),
        in_specs=[vmem],
        out_specs=(vmem,) * 6,
        scratch_shapes=[pltpu.VMEM((width + 2 * EXT, 4 * width), f32)],
        compiler_params=pltpu.CompilerParams(vmem_limit_bytes=16 << 20),
    )(got)
    return (mixed[None], gtok[None], dgain[0], dnb[0], dwq, dbq[0], dwp, dbp[0])


def solution(mesh):
    split = P("clip", "frame", None, None, None)
    in_specs = (split, P("clip"), P(), P(), P(), P(), P(), P(), split)
    out_specs = (split, split, P(), P(), P(), P(), P(), P())
    return jax.shard_map(
        per_device, mesh=mesh, in_specs=in_specs, out_specs=out_specs, check_vma=False
    )
```

time: 113 us -> 88.9 us (0.79)
  blocking collectives: 35.8 us -> 16.2 us
  waiting for transfers between devices: 29.4 us -> 14.2 us
  starting transfers between devices: 17.6 us -> 29.3 us
  Pallas kernels: 21.8 us -> 20.3 us
    ppermute x2 -> x4, waiting for transfers between devices: 24.9 us -> 0.01 us  [swapped(): return lax.ppermute(array, 'frame', pairs)]
    all_to_all x2 -> x1, blocking collectives: 35.8 us -> 16.2 us  [exchange(): lax.all_to_all(x, AXES, 0, 0, tiled=True, axis_index_groups=groups_of(bit...]
    all_to_all x1 -> x2, waiting for transfers between devices: 4.44 us -> 14.2 us  [exchange(): lax.all_to_all(x, AXES, 0, 0, tiled=True, axis_index_groups=groups_of(bit...]
    all_to_all x1 -> x2, starting transfers between devices: 5.88 us -> 13.2 us  [exchange(): lax.all_to_all(x, AXES, 0, 0, tiled=True, axis_index_groups=groups_of(bit...]
    ppermute x2 -> x4, starting transfers between devices: 11.7 us -> 16.1 us  [swapped(): return lax.ppermute(array, 'frame', pairs)]
    dynamic_slice x0 -> x3, local copies, waits for them, and re-layouts: none -> 1.62 us  [per_device(): lax.dynamic_slice(a, at, size)[0, :, 0][None]]
    pallas_call x2 -> x5, Pallas kernels: 21.8 us -> 20.3 us  [the longest x2 19.1 us: block(): pl.pallas_call(functools.partial(block_kernel, frame_total, last), name='...]
    unnamed x26 -> x20, local copies, waits for them, and re-layouts: 3.15 us -> 2.63 us
  transfers between devices with their start and end apart: 3 -> 6, of which waited for: 3 -> 2; matrix products, arithmetic and copies ran while one was open for 1% -> 4% of each run, Pallas kernels for 0% -> 22%
where the time goes in v2:
time: 88.9 us; the launch traced here: 88.6 us
  starting transfers between devices  29.3 us (33%)
  Pallas kernels  20.3 us (23%)
  blocking collectives  16.2 us (18%)
  waiting for transfers between devices  14.2 us (16%)
  local copies, waits for them, and re-layouts  6.25 us (7%)
  between operations  1.55 us (2%)
    pallas_call x2, Pallas kernels, block(): pl.pallas_call(functools.partial(block_kernel, frame_total, last), name='...  19.1 us
    all_to_all x1, blocking collectives, exchange(): lax.all_to_all(x, AXES, 0, 0, tiled=True, axis_index_groups=groups_of(bit...  16.2 us
    ppermute x4, starting transfers between devices, swapped(): return lax.ppermute(array, 'frame', pairs)  16.1 us
    all_to_all x2, waiting for transfers between devices, exchange(): lax.all_to_all(x, AXES, 0, 0, tiled=True, axis_index_groups=groups_of(bit...  14.2 us
    all_to_all x2, starting transfers between devices, exchange(): lax.all_to_all(x, AXES, 0, 0, tiled=True, axis_index_groups=groups_of(bit...  13.2 us
    unnamed x20, local copies, waits for them, and re-layouts  2.63 us
  transfers between devices with their start and end apart: 6, of which 2 were waited for; matrix products, arithmetic and copies ran while one was open for 4% of the time, Pallas kernels for 22%

profile of v2, /device:TPU:1, one launch (start us, length us, event | category | flops | bytes accessed | tf_op | source)
XLA Modules:
  0.0 88.6 jit_solution(11888199942917907473)
XLA Ops:
  0.6 0.0 copy-start.3
  0.6 0.0 copy-start.4
  0.7 1.5 %constant_dynamic-slice_fusion = (bf16[1,4,1,49,256]{4,2,3,1,0:T(2,128)(2,1)S(1)}, bf16[1,4,1,49,256]{4,2,3,1,0:T(2,128)(2,1)S(1)}) fusion(bf16[1,8,2,49,256]{4,2,3,1,0:T(2,128)(2,1)} %param.17, s32[]{:T(128)S(6)} %select_n.13, s32[]{:T(128)S(6)} %select_n.15, bf16[1,8,2,49,256]{4,2,3,1,0:T(2,128)(2,1)} %param.9), kind=kLoop, calls=%fused_computation.5 | loop fusion | bytes 401416 | tf_op jit(solution)/shard_map/dynamic_slice | solution.py:254
  2.2 0.1 copy.59
  2.3 0.1 copy.60
  2.4 0.0 copy-start.7
  2.4 0.0 copy-start.6
  2.4 2.6 %collective-permute-start = (bf16[2,4,49,256]{3,2,1,0:T(8,128)(2,1)S(1)}, bf16[2,4,49,256]{3,2,1,0:T(8,128)(2,1)S(1)}, u32[]{:S(2)}, u32[]{:S(2)}) collective-permute-start(bf16[2,4,49,256]{3,2,1,0:T(8,128)(2,1)S(1)} %pad_maximum_fusion), channel_id=1, source_target_pairs={{0,4},{4,0},{8,12},{12,8},{16,20},{20,16},{24,28},{28,24},{32,36},... | collective-permute-start | bytes 602120 | tf_op jit(solution)/shard_map/ppermute | solution.py:24
  5.0 0.0 copy-done.3
  5.0 0.0 copy-done.4
  5.0 0.1 copy_bitcast_fusion
  5.1 0.0 copy-start.5
  5.2 9.7 %collective-permute-start.1 = (bf16[2,4,49,256]{3,2,1,0:T(8,128)(2,1)S(1)}, bf16[2,4,49,256]{3,2,1,0:T(8,128)(2,1)S(1)}, u32[]{:S(2)}, u32[]{:S(2)}) collective-permute-start(bf16[2,4,49,256]{3,2,1,0:T(8,128)(2,1)S(1)} %pick.1), channel_id=1, source_target_pairs={{0,252},{4,8},{8,4},{12,16},{16,12},{20,24},{24,20},{28,32},{32,28... | collective-permute-start | bytes 602120 | tf_op jit(solution)/shard_map/ppermute | solution.py:24
  15.5 0.0 copy-done.7
  15.5 0.0 copy-done.6
  15.5 0.1 copy.48
  15.6 0.0 copy-start
  15.6 0.0 copy-start.1
  15.6 0.0 copy-start.2
  15.6 0.1 copy.50.wp
  15.8 0.0 copy-done.5
  15.8 0.2 copy.47
  15.9 0.2 copy.49.w
  16.1 0.0 collective-permute-done.halo
  16.1 0.2 copy-done
  16.3 0.0 copy-done.1
  16.3 0.0 copy-done.2
  16.3 9.6 %first_window.1 = (bf16[4,49,256]{2,1,0:T(8,128)(2,1)S(1)}, bf16[4,49,256]{2,1,0:T(8,128)(2,1)S(1)}, bf16[2,4,49,256]{3,2,1,0:T(8,128)(2,1)S(1)}, f32[288,1024]{1,0:T(8,128)S(1)}) custom-call(s32[1]{0:T(128)S(6)} %copy.61.lengths, bf16[8,2,49,256]{3,2,1,0:T(8,128)(2,1)S(1)} %get-tuple-element.71.tok, bf16[8,2,49,256]{3,2,1,0:T(8,128)(2,1)S(1)} %get-tuple-element.70.gr, ...), custom_call_target="tpu_custom_call" | custom-call | flops 8000000000 | bytes 8000000 | tf_op jit(solution)/shard_map/first_window/pallas_call | solution.py:275
  25.9 0.1 collective-permute-start.2
  26.0 0.0 collective-permute-done.1.halo
  26.0 9.6 %second_window.1 = (bf16[4,49,256]{2,1,0:T(8,128)(2,1)S(1)}, bf16[4,49,256]{2,1,0:T(8,128)(2,1)S(1)}, bf16[2,4,49,256]{3,2,1,0:T(8,128)(2,1)S(1)}, bf16[32,72,128]{2,1,0:T(8,128)(2,1)S(1)}) custom-call(s32[1]{0:T(128)S(6)} %copy.61.lengths, bf16[8,2,49,256]{3,2,1,0:T(8,128)(2,1)S(1)} %get-tuple-element.71.tok, ...), custom_call_target="tpu_custom_call" | custom-call | flops 8000000000 | bytes 8000000 | tf_op jit(solution)/shard_map/second_window/pallas_call | solution.py:275
  35.6 0.0 collective-permute-done.2.back1
  35.6 16.2 %all_to_all.15 = bf16[32,72,128]{2,1,0:T(8,128)(2,1)S(1)} all-to-all(bf16[32,72,128]{2,1,0:T(8,128)(2,1)S(1)} %get-tuple-element.37), channel_id=1, replica_groups={{0,1,2,3,32,33,34,35,64,65,66,67,96,97,98,99,128,129,130,131,160,161,16..., dimensions={0} | all-to-all | bytes 1179648 | tf_op jit(solution)/shard_map/all_to_all | solution.py:228
  51.8 0.1 reduce_sum.24
  51.9 0.7 broadcast_in_dim.34
  52.6 7.1 %all-to-all-start.1 = ((bf16[8,72,128]{2,1,0:T(8,128)(2,1)}), bf16[8,72,128]{2,1,0:T(8,128)(2,1)S(1)}, u32[]{:S(2)}, u32[]{:S(2)}) async-start(bf16[8,72,128]{2,1,0:T(8,128)(2,1)} %broadcast_in_dim.34), calls=%async_computation.1 | async-start | bytes 294912 | tf_op jit(solution)/shard_map/all_to_all | solution.py:228
  59.7 3.8 %collective-permute-start.3 = (bf16[2,4,49,256]{3,2,1,0:T(8,128)(2,1)S(1)}, bf16[2,4,49,256]{3,2,1,0:T(8,128)(2,1)S(1)}, u32[]{:S(2)}, u32[]{:S(2)}) collective-permute-start(bf16[2,4,49,256]{3,2,1,0:T(8,128)(2,1)S(1)} %get-tuple-element.34), channel_id=1, source_target_pairs={{0,252},{4,8},{8,4},{12,16},{16,12},{20,24},{24,20},{28,32},{32,28... | collective-permute-start | bytes 602120 | tf_op jit(solution)/shard_map/ppermute | solution.py:24
  63.5 4.2 %all-to-all-done.1 = bf16[8,72,128]{2,1,0:T(8,128)(2,1)S(1)} async-done(((bf16[8,72,128]{2,1,0:T(8,128)(2,1)}), bf16[8,72,128]{2,1,0:T(8,128)(2,1)S(1)}, u32[]{:S(2)}, u32[]{:S(2)}) %all-to-all-start.1) | async-done | bytes 147488 | tf_op jit(solution)/shard_map/all_to_all | solution.py:228
  67.8 0.9 %broadcast_in_dim.35 = bf16[32,72,128]{2,1,0:T(8,128)(2,1)} broadcast(bf16[72,128]{1,0:T(8,128)(2,1)S(1)} %reduce_sum.25), dimensions={1,2} | broadcast | bytes 608256 | tf_op jit(solution)/shard_map/broadcast_in_dim | solution.py:311
  68.6 6.1 %all-to-all-start.2 = ((bf16[32,72,128]{2,1,0:T(8,128)(2,1)}), bf16[32,72,128]{2,1,0:T(8,128)(2,1)S(1)}, u32[]{:S(2)}, u32[]{:S(2)}) async-start(bf16[32,72,128]{2,1,0:T(8,128)(2,1)} %broadcast_in_dim.35), calls=%async_computation.2 | async-start | bytes 1179648 | tf_op jit(solution)/shard_map/all_to_all | solution.py:228
  74.7 0.0 collective-permute-done.3.back2
  74.8 0.1 join.1
  74.9 1.1 %copy.53 = bf16[1,8,2,49,256]{4,2,3,1,0:T(2,128)(2,1)} copy(bf16[1,8,2,49,256]{4,3,2,1,0:T(8,128)(2,1)S(1)} %bitcast.25) | data formatting | bytes 802816
  76.0 1.1 %copy.54 = bf16[1,8,2,49,256]{4,2,3,1,0:T(2,128)(2,1)} copy(bf16[1,8,2,49,256]{4,3,2,1,0:T(8,128)(2,1)S(1)} %bitcast.24) | data formatting | bytes 802816
  77.0 10.0 %all-to-all-done.2.got = bf16[32,72,128]{2,1,0:T(8,128)(2,1)S(1)} async-done(((bf16[32,72,128]{2,1,0:T(8,128)(2,1)}), bf16[32,72,128]{2,1,0:T(8,128)(2,1)S(1)}, u32[]{:S(2)}, u32[]{:S(2)}) %all-to-all-start.2) | async-done | bytes 589856 | tf_op jit(solution)/shard_map/all_to_all | solution.py:228
  87.0 1.0 %unpack.1 = (f32[1,256]{1,0:T(1,128)}, f32[1,256]{1,0:T(1,128)}, f32[256,768]{1,0:T(8,128)}, f32[1,768]{1,0:T(1,128)S(1)}, f32[256,256]{1,0:T(8,128)}, /*index=5*/f32[1,256]{1,0:T(1,128)}) custom-call(bf16[32,72,128]{2,1,0:T(8,128)(2,1)S(1)} %all-to-all-done.2.got), custom_call_target="tpu_custom_call" | custom-call | tf_op jit(solution)/shard_map/unpack/pallas_call | solution.py:327
  88.0 0.6 reduce.2
  (6 shorter events, 0.1 us)
Async XLA Ops:
  0.6 4.3 %copy-start.3 = (bf16[1,8,2,49,256]{4,2,3,1,0:T(2,128)(2,1)S(1)}, bf16[1,8,2,49,256]{4,2,3,1,0:T(2,128)(2,1)}, u32[]{:S(2)}) copy-start(bf16[1,8,2,49,256]{4,2,3,1,0:T(2,128)(2,1)} %param.17) | copy-start | bytes 1204228
  0.6 4.3 %copy-start.4 = (bf16[1,8,2,49,256]{4,2,3,1,0:T(2,128)(2,1)S(1)}, bf16[1,8,2,49,256]{4,2,3,1,0:T(2,128)(2,1)}, u32[]{:S(2)}) copy-start(bf16[1,8,2,49,256]{4,2,3,1,0:T(2,128)(2,1)} %param.9) | copy-start | bytes 1204228
  2.4 13.1 %copy-start.7 = (f32[768]{0:T(1024)S(1)}, f32[768]{0:T(1024)}, u32[]{:S(2)}) copy-start(f32[768]{0:T(1024)} %param.14) | copy-start | bytes 9220
  2.4 13.1 %copy-start.6 = (f32[256,256]{1,0:T(8,128)S(1)}, f32[256,256]{1,0:T(8,128)}, u32[]{:S(2)}) copy-start(f32[256,256]{1,0:T(8,128)} %param.15) | copy-start | bytes 786436
  2.4 13.7 %collective-permute-start = (bf16[2,4,49,256]{3,2,1,0:T(8,128)(2,1)S(1)}, bf16[2,4,49,256]{3,2,1,0:T(8,128)(2,1)S(1)}, u32[]{:S(2)}, u32[]{:S(2)}) collective-permute-start(bf16[2,4,49,256]{3,2,1,0:T(8,128)(2,1)S(1)} %pad_maximum_fusion), channel_id=1, source_target_pairs={{0,4},{4,0},{8,12},{12,8},{16,20},{20,16},{24,28},{28,24},{32,36},... | collective-permute-start | bytes 602120 | tf_op jit(solution)/shard_map/ppermute | solution.py:24
  5.1 10.7 %copy-start.5 = (f32[256,768]{1,0:T(8,128)S(1)}, f32[256,768]{1,0:T(8,128)}, u32[]{:S(2)}) copy-start(f32[256,768]{1,0:T(8,128)} %param.13) | copy-start | bytes 2359300
  5.2 20.8 %collective-permute-start.1 = (bf16[2,4,49,256]{3,2,1,0:T(8,128)(2,1)S(1)}, bf16[2,4,49,256]{3,2,1,0:T(8,128)(2,1)S(1)}, u32[]{:S(2)}, u32[]{:S(2)}) collective-permute-start(bf16[2,4,49,256]{3,2,1,0:T(8,128)(2,1)S(1)} %pick.1), channel_id=1, source_target_pairs={{0,252},{4,8},{8,4},{12,16},{16,12},{20,24},{24,20},{28,32},{32,28... | collective-permute-start | bytes 602120 | tf_op jit(solution)/shard_map/ppermute | solution.py:24
  15.6 0.7 copy-start
  15.6 0.7 copy-start.1
  15.6 0.7 copy-start.2
  25.9 9.7 %collective-permute-start.2 = (bf16[2,4,49,256]{3,2,1,0:T(8,128)(2,1)S(1)}, bf16[2,4,49,256]{3,2,1,0:T(8,128)(2,1)S(1)}, u32[]{:S(2)}, u32[]{:S(2)}) collective-permute-start(bf16[2,4,49,256]{3,2,1,0:T(8,128)(2,1)S(1)} %get-tuple-element.30), channel_id=1, source_target_pairs={{0,4},{4,0},{8,12},{12,8},{16,20},{20,16},{24,28},{28,24},{32,36},... | collective-permute-start | bytes 602120 | tf_op jit(solution)/shard_map/ppermute | solution.py:24
  52.6 15.1 %all-to-all-start.1 = ((bf16[8,72,128]{2,1,0:T(8,128)(2,1)}), bf16[8,72,128]{2,1,0:T(8,128)(2,1)S(1)}, u32[]{:S(2)}, u32[]{:S(2)}) async-start(bf16[8,72,128]{2,1,0:T(8,128)(2,1)} %broadcast_in_dim.34), calls=%async_computation.1 | async-start | bytes 294912 | tf_op jit(solution)/shard_map/all_to_all | solution.py:228
  59.7 15.0 %collective-permute-start.3 = (bf16[2,4,49,256]{3,2,1,0:T(8,128)(2,1)S(1)}, bf16[2,4,49,256]{3,2,1,0:T(8,128)(2,1)S(1)}, u32[]{:S(2)}, u32[]{:S(2)}) collective-permute-start(bf16[2,4,49,256]{3,2,1,0:T(8,128)(2,1)S(1)} %get-tuple-element.34), channel_id=1, source_target_pairs={{0,252},{4,8},{8,4},{12,16},{16,12},{20,24},{24,20},{28,32},{32,28... | collective-permute-start | bytes 602120 | tf_op jit(solution)/shard_map/ppermute | solution.py:24
  68.6 18.3 %all-to-all-start.2 = ((bf16[32,72,128]{2,1,0:T(8,128)(2,1)}), bf16[32,72,128]{2,1,0:T(8,128)(2,1)S(1)}, u32[]{:S(2)}, u32[]{:S(2)}) async-start(bf16[32,72,128]{2,1,0:T(8,128)(2,1)} %broadcast_in_dim.35), calls=%async_computation.2 | async-start | bytes 1179648 | tf_op jit(solution)/shard_map/all_to_all | solution.py:228

commit v3 on v2

--- a/solution.py
+++ b/solution.py
@@ -13,7 +13,7 @@
 HALF = WT // 2
 AXES = ("frame", "clip")
 BIG = 2.0**100
-UNROLL = 2
+UNROLL = 8
 EXT = 16
 f32, bf16 = jnp.float32, jnp.bfloat16
 
@@ -43,13 +43,15 @@
 
 
 def block_kernel(
-    frame_total, last, lengths, tok, gr, halo, gain, nb, w, wT, wp, wpT, bq, bp, *refs
+    frame_total, last, lengths, tok, gr, halo, gain, nb, w32, wp32, bq, bp, *refs
 ):
     if last:
         acc_in, mixed, gtok, send, pay = refs[:5]
     else:
         mixed, gtok, send, acc_out = refs[:4]
-    xs, gs, normT, gN, qkvT, doT, attT, dqT, acc, ext = refs[-10:]
+    xs, gs, normT, gN, qkvT, doT, attT, dqT, acc, ext, w, wp = refs[-12:]
+    w[...] = w32[...].astype(bf16)
+    wp[...] = wp32[...].astype(bf16)
     patch, width = tok.shape[2:]
     rows = WT * patch
     depth = width // HEADS
@@ -104,7 +106,7 @@
     normT[:width, :] = jnp.transpose(normed).astype(bf16)
     normT[width:, :] = one_row
     attT[width:, :] = one_row
-    qkvT[...] = (mm(wT[...], normT[:width, :]) + bqT).astype(bf16)
+    qkvT[...] = (mm(w[...], normT[:width, :], 0, 0) + bqT).astype(bf16)
     gN[...] = gs[...].astype(bf16)
     doT[...] = mm(wp[...], gN[...], 1, 1).astype(bf16)
 
@@ -146,7 +148,7 @@
     wide = 3 * width
     acc[: width + EXT, :wide] = mm(normT[...], dqT[...], 1, 1)
     acc[: width + EXT, wide:] = mm(attT[...], gN[...])
-    gs[...] = jnp.transpose(mm(wpT[...], attT[:width, :])) + bp[...]
+    gs[...] = jnp.transpose(mm(wp[...], attT[:width, :], 0, 0)) + bp[...]
     for u in range(WT):
         k = u % HALF
         b_u = (gs[pl.ds(u * patch, patch), :] * valid_of(u)).astype(bf16)
@@ -201,6 +203,27 @@
             ).astype(bf16)
 
 
+def spread_kernel(parts, out):
+    total = parts[0].astype(f32)
+    for k in range(1, parts.shape[0]):
+        total = total + parts[k].astype(f32)
+    total = total.astype(bf16)
+    for k in range(out.shape[0]):
+        out[k] = total
+
+
+def spread(parts, copies):
+    vmem = pl.BlockSpec(memory_space=pltpu.VMEM)
+    return pl.pallas_call(
+        spread_kernel,
+        name="spread",
+        out_shape=jax.ShapeDtypeStruct((copies,) + parts.shape[1:], bf16),
+        in_specs=[vmem],
+        out_specs=vmem,
+        compiler_params=pltpu.CompilerParams(vmem_limit_bytes=8 << 20),
+    )(parts)
+
+
 def unpack_kernel(width, got, dgain, dnb, dwq, dbq, dwp, dbp, full):
     chunks, deep, lanes = got.shape
     across = 4 * width // lanes
@@ -209,10 +232,10 @@
         full[r * deep : (r + 1) * deep, k * lanes : (k + 1) * lanes] = got[c].astype(f32)
     dwq[...] = full[:width, : 3 * width]
     dwp[...] = full[:width, 3 * width :]
-    dbq[...] = full[width : width + 1, : 3 * width]
-    dbp[...] = full[width : width + 1, 3 * width :]
-    dgain[...] = full[width + EXT : width + EXT + 1, :width]
-    dnb[...] = full[width + EXT : width + EXT + 1, width : 2 * width]
+    dbq[...] = full[width, : 3 * width]
+    dbp[...] = full[width, 3 * width :]
+    dgain[...] = full[width + EXT, :width]
+    dnb[...] = full[width + EXT, width : 2 * width]
 
 
 def groups_of(bits, devices):
@@ -263,8 +286,6 @@
         compiler_params=pltpu.CompilerParams(vmem_limit_bytes=8 << 20),
     )(tok, gr)
     halo2 = swapped(give2, 1)
-    w = qkv_weight.astype(bf16)
-    wp = proj_weight.astype(bf16)
     near = 1 << len(NEAR)
     deep = (width + 2 * EXT) * 4 * width // 128 // near
     total_rows = width + 2 * EXT
@@ -276,7 +297,7 @@
             functools.partial(block_kernel, frame_total, last),
             name="second_window" if last else "first_window",
             out_shape=(half, half, halves, pay_type if last else sums_type),
-            in_specs=[smem] + [vmem] * (11 + len(more)),
+            in_specs=[smem] + [vmem] * (9 + len(more)),
             out_specs=(vmem,) * 4,
             scratch_shapes=[
                 pltpu.VMEM((rows, width), f32),
@@ -289,26 +310,26 @@
                 pltpu.VMEM((3 * width, rows), bf16),
                 pltpu.VMEM((total_rows, 4 * width), f32),
                 pltpu.VMEM((2, EXT, rows), bf16),
+                pltpu.VMEM((width, 3 * width), bf16),
+                pltpu.VMEM((width, width), bf16),
             ],
             compiler_params=pltpu.CompilerParams(vmem_limit_bytes=32 << 20),
             cost_estimate=pl.CostEstimate(
                 flops=8_000_000_000, bytes_accessed=8_000_000, transcendentals=2_000_000
             ),
         )(
-            lengths, tok, gr, halo, norm_gain[None], norm_bias[None], w, w.T, wp, wp.T,
-            qkv_bias[None], proj_bias[None], *more,
+            lengths, tok, gr, halo, norm_gain[None], norm_bias[None], qkv_weight,
+            proj_weight, qkv_bias[None], proj_bias[None], *more,
         )
 
     mixed1, gtok1, send1, sums1 = block(False, halo1)
     back1 = swapped(send1, 0)
     mixed2, gtok2, send2, pay = block(True, halo2, sums1)
     pay, back1 = lax.optimization_barrier((pay, back1))
-    part = jnp.sum(exchange(pay, NEAR).astype(f32), axis=0).astype(bf16)
-    deeper = 1 << len(ALONG_Z)
-    sums = exchange(jnp.broadcast_to(part, (deeper,) + part.shape), ALONG_Z)
-    total = jnp.sum(sums.astype(f32), axis=0).astype(bf16)
     back2 = swapped(send2, 1)
-    got = exchange(jnp.broadcast_to(total, (near,) + part.shape), NEAR)
+    part = spread(exchange(pay, NEAR), 1 << len(ALONG_Z))
+    total = spread(exchange(part, ALONG_Z), near)
+    got = exchange(total, NEAR)
     slab = jax.ShapeDtypeStruct(tok.shape, bf16)
     mixed, gtok = pl.pallas_call(
         join_kernel,
@@ -328,19 +349,19 @@
         functools.partial(unpack_kernel, width),
         name="unpack",
         out_shape=(
-            jax.ShapeDtypeStruct((1, width), f32),
-            jax.ShapeDtypeStruct((1, width), f32),
+            jax.ShapeDtypeStruct((width,), f32),
+            jax.ShapeDtypeStruct((width,), f32),
             jax.ShapeDtypeStruct((width, 3 * width), f32),
-            jax.ShapeDtypeStruct((1, 3 * width), f32),
+            jax.ShapeDtypeStruct((3 * width,), f32),
             jax.ShapeDtypeStruct((width, width), f32),
-            jax.ShapeDtypeStruct((1, width), f32),
+            jax.ShapeDtypeStruct((width,), f32),
         ),
         in_specs=[vmem],
         out_specs=(vmem,) * 6,
         scratch_shapes=[pltpu.VMEM((width + 2 * EXT, 4 * width), f32)],
         compiler_params=pltpu.CompilerParams(vmem_limit_bytes=16 << 20),
     )(got)
-    return (mixed[None], gtok[None], dgain[0], dnb[0], dwq, dbq[0], dwp, dbp[0])
+    return (mixed[None], gtok[None], dgain, dnb, dwq, dbq, dwp, dbp)
 
 
 def solution(mesh):

time: 88.9 us -> 87.4 us (0.983)
  local copies, waits for them, and re-layouts: 6.25 us -> 3.95 us
    pallas_call x0 -> x2, Pallas kernels: none -> 1.62 us  [spread(): pl.pallas_call(spread_kernel, name='spread', out_shape=jax.ShapeDtypeStru...]
    broadcast_in_dim x2 -> x0, local copies, waits for them, and re-layouts: 1.57 us -> none  [the longest x1 0.89 us: per_device(): got = exchange(jnp.broadcast_to(total, (near,) + part.shape), NEAR)]
    pallas_call x2, Pallas kernels: 19.1 us -> 18 us  [block(): pl.pallas_call(functools.partial(block_kernel, frame_total, last), name='...]
    unnamed x20 -> x18, local copies, waits for them, and re-layouts: 2.63 us -> 2.17 us
  transfers between devices with their start and end apart: 6 -> 6, of which waited for: 2 -> 2; matrix products, arithmetic and copies ran while one was open for 4% -> 3% of each run, Pallas kernels for 22% -> 22%
where the time goes in v3:
time: 87.4 us; the launch traced here: 87.1 us
  starting transfers between devices  29.6 us (34%)
  Pallas kernels  20.8 us (24%)
  blocking collectives  16.9 us (19%)
  waiting for transfers between devices  14.2 us (16%)
  local copies, waits for them, and re-layouts  3.95 us (5%)
  between operations  1.54 us (2%)
    pallas_call x2, Pallas kernels, block(): pl.pallas_call(functools.partial(block_kernel, frame_total, last), name='...  18 us
    all_to_all x1, blocking collectives, exchange(): lax.all_to_all(x, AXES, 0, 0, tiled=True, axis_index_groups=groups_of(bit...  16.9 us
    ppermute x4, starting transfers between devices, swapped(): return lax.ppermute(array, 'frame', pairs)  16.3 us
    all_to_all x2, waiting for transfers between devices, exchange(): lax.all_to_all(x, AXES, 0, 0, tiled=True, axis_index_groups=groups_of(bit...  14.2 us
    all_to_all x2, starting transfers between devices, exchange(): lax.all_to_all(x, AXES, 0, 0, tiled=True, axis_index_groups=groups_of(bit...  13.4 us
    unnamed x18, local copies, waits for them, and re-layouts  2.17 us
  transfers between devices with their start and end apart: 6, of which 2 were waited for; matrix products, arithmetic and copies ran while one was open for 3% of the time, Pallas kernels for 22%

profile of v3, /device:TPU:1, one launch (start us, length us, event | category | flops | bytes accessed | tf_op | source)
XLA Modules:
  0.0 87.1 jit_solution(18422897871429236511)
XLA Ops:
  0.6 0.0 copy-start.5
  0.6 0.0 copy-start.6
  0.7 1.5 %constant_dynamic-slice_fusion = (bf16[1,4,1,49,256]{4,2,3,1,0:T(2,128)(2,1)S(1)}, bf16[1,4,1,49,256]{4,2,3,1,0:T(2,128)(2,1)S(1)}) fusion(bf16[1,8,2,49,256]{4,2,3,1,0:T(2,128)(2,1)} %param.17, s32[]{:T(128)S(6)} %select_n.13, s32[]{:T(128)S(6)} %select_n.15, bf16[1,8,2,49,256]{4,2,3,1,0:T(2,128)(2,1)} %param.9), kind=kLoop, calls=%fused_computation.5 | loop fusion | bytes 401416 | tf_op jit(solution)/shard_map/dynamic_slice | solution.py:277
  2.2 0.1 copy.33
  2.3 0.1 copy.34
  2.4 0.0 copy-start.7
  2.4 0.0 copy-start
  2.4 0.0 copy-start.1
  2.4 0.0 copy-start.2
  2.4 0.0 copy-start.3
  2.4 0.0 copy-start.4
  2.5 2.6 %collective-permute-start = (bf16[2,4,49,256]{3,2,1,0:T(8,128)(2,1)S(1)}, bf16[2,4,49,256]{3,2,1,0:T(8,128)(2,1)S(1)}, u32[]{:S(2)}, u32[]{:S(2)}) collective-permute-start(bf16[2,4,49,256]{3,2,1,0:T(8,128)(2,1)S(1)} %pad_maximum_fusion), channel_id=1, source_target_pairs={{0,4},{4,0},{8,12},{12,8},{16,20},{20,16},{24,28},{28,24},{32,36},... | collective-permute-start | bytes 602120 | tf_op jit(solution)/shard_map/ppermute | solution.py:24
  5.0 0.0 copy-done.5
  5.0 0.0 copy-done.6
  5.0 0.1 copy_bitcast_fusion
  5.2 9.7 %collective-permute-start.1 = (bf16[2,4,49,256]{3,2,1,0:T(8,128)(2,1)S(1)}, bf16[2,4,49,256]{3,2,1,0:T(8,128)(2,1)S(1)}, u32[]{:S(2)}, u32[]{:S(2)}) collective-permute-start(bf16[2,4,49,256]{3,2,1,0:T(8,128)(2,1)S(1)} %pick.1), channel_id=1, source_target_pairs={{0,252},{4,8},{8,4},{12,16},{16,12},{20,24},{24,20},{28,32},{32,28... | collective-permute-start | bytes 602120 | tf_op jit(solution)/shard_map/ppermute | solution.py:24
  15.5 0.0 copy-done.7
  15.5 0.0 collective-permute-done.halo
  15.5 0.0 copy-done
  15.5 0.0 copy-done.1
  15.6 0.0 copy-done.2
  15.6 0.0 copy-done.3
  15.6 0.0 copy-done.4
  15.6 9.0 %first_window.1 = (bf16[4,49,256]{2,1,0:T(8,128)(2,1)S(1)}, bf16[4,49,256]{2,1,0:T(8,128)(2,1)S(1)}, bf16[2,4,49,256]{3,2,1,0:T(8,128)(2,1)S(1)}, f32[288,1024]{1,0:T(8,128)S(1)}) custom-call(s32[1]{0:T(128)S(6)} %copy.35.lengths, bf16[8,2,49,256]{3,2,1,0:T(8,128)(2,1)S(1)} %get-tuple-element.63.tok, bf16[8,2,49,256]{3,2,1,0:T(8,128)(2,1)S(1)} %get-tuple-element.62.gr, ...), custom_call_target="tpu_custom_call" | custom-call | flops 8000000000 | bytes 8000000 | tf_op jit(solution)/shard_map/first_window/pallas_call | solution.py:296
  24.6 0.3 collective-permute-start.2
  24.8 0.0 collective-permute-done.1.halo
  24.9 9.0 %second_window.1 = (bf16[4,49,256]{2,1,0:T(8,128)(2,1)S(1)}, bf16[4,49,256]{2,1,0:T(8,128)(2,1)S(1)}, bf16[2,4,49,256]{3,2,1,0:T(8,128)(2,1)S(1)}, bf16[32,72,128]{2,1,0:T(8,128)(2,1)S(1)}) custom-call(s32[1]{0:T(128)S(6)} %copy.35.lengths, bf16[8,2,49,256]{3,2,1,0:T(8,128)(2,1)S(1)} %get-tuple-element.63.tok, ...), custom_call_target="tpu_custom_call" | custom-call | flops 8000000000 | bytes 8000000 | tf_op jit(solution)/shard_map/second_window/pallas_call | solution.py:296
  33.9 0.0 collective-permute-done.2.back1
  33.9 16.9 %all_to_all.15.parts = bf16[32,72,128]{2,1,0:T(8,128)(2,1)S(1)} all-to-all(bf16[32,72,128]{2,1,0:T(8,128)(2,1)S(1)} %get-tuple-element.37), channel_id=1, replica_groups={{0,1,2,3,32,33,34,35,64,65,66,67,96,97,98,99,128,129,130,131,160,161,16..., dimensions={0} | all-to-all | bytes 1179648 | tf_op jit(solution)/shard_map/all_to_all | solution.py:251
  50.7 0.8 spread.2
  51.5 7.3 %all-to-all-start.1 = ((bf16[8,72,128]{2,1,0:T(8,128)(2,1)}), bf16[8,72,128]{2,1,0:T(8,128)(2,1)S(1)}, u32[]{:S(2)}, u32[]{:S(2)}) async-start(bf16[8,72,128]{2,1,0:T(8,128)(2,1)} %spread.2), calls=%async_computation.1 | async-start | bytes 294912 | tf_op jit(solution)/shard_map/all_to_all | solution.py:251
  58.8 3.8 %collective-permute-start.3 = (bf16[2,4,49,256]{3,2,1,0:T(8,128)(2,1)S(1)}, bf16[2,4,49,256]{3,2,1,0:T(8,128)(2,1)S(1)}, u32[]{:S(2)}, u32[]{:S(2)}) collective-permute-start(bf16[2,4,49,256]{3,2,1,0:T(8,128)(2,1)S(1)} %get-tuple-element.34), channel_id=1, source_target_pairs={{0,252},{4,8},{8,4},{12,16},{16,12},{20,24},{24,20},{28,32},{32,28... | collective-permute-start | bytes 602120 | tf_op jit(solution)/shard_map/ppermute | solution.py:24
  62.5 4.2 %all-to-all-done.1.parts = bf16[8,72,128]{2,1,0:T(8,128)(2,1)S(1)} async-done(((bf16[8,72,128]{2,1,0:T(8,128)(2,1)}), bf16[8,72,128]{2,1,0:T(8,128)(2,1)S(1)}, u32[]{:S(2)}, u32[]{:S(2)}) %all-to-all-start.1) | async-done | bytes 147488 | tf_op jit(solution)/shard_map/all_to_all | solution.py:251
  66.8 0.9 spread.3
  67.6 6.1 %all-to-all-start.2 = ((bf16[32,72,128]{2,1,0:T(8,128)(2,1)}), bf16[32,72,128]{2,1,0:T(8,128)(2,1)S(1)}, u32[]{:S(2)}, u32[]{:S(2)}) async-start(bf16[32,72,128]{2,1,0:T(8,128)(2,1)} %spread.3), calls=%async_computation.2 | async-start | bytes 1179648 | tf_op jit(solution)/shard_map/all_to_all | solution.py:251
  73.7 0.0 collective-permute-done.3.back2
  73.8 0.1 join.1
  73.9 1.1 %copy.27 = bf16[1,8,2,49,256]{4,2,3,1,0:T(2,128)(2,1)} copy(bf16[1,8,2,49,256]{4,3,2,1,0:T(8,128)(2,1)S(1)} %bitcast.16) | data formatting | bytes 802816
  75.0 1.1 %copy.28 = bf16[1,8,2,49,256]{4,2,3,1,0:T(2,128)(2,1)} copy(bf16[1,8,2,49,256]{4,3,2,1,0:T(8,128)(2,1)S(1)} %bitcast.15) | data formatting | bytes 802816
  76.0 10.0 %all-to-all-done.2.got = bf16[32,72,128]{2,1,0:T(8,128)(2,1)S(1)} async-done(((bf16[32,72,128]{2,1,0:T(8,128)(2,1)}), bf16[32,72,128]{2,1,0:T(8,128)(2,1)S(1)}, u32[]{:S(2)}, u32[]{:S(2)}) %all-to-all-start.2) | async-done | bytes 589856 | tf_op jit(solution)/shard_map/all_to_all | solution.py:251
  86.0 1.1 %unpack.1 = (f32[256]{0:T(256)}, f32[256]{0:T(256)}, f32[256,768]{1,0:T(8,128)}, f32[768]{0:T(1024)}, f32[256,256]{1,0:T(8,128)}, /*index=5*/f32[256]{0:T(256)}) custom-call(bf16[32,72,128]{2,1,0:T(8,128)(2,1)S(1)} %all-to-all-done.2.got), custom_call_target="tpu_custom_call" | custom-call | tf_op jit(solution)/shard_map/unpack/pallas_call | solution.py:348
  (5 shorter events, 0.1 us)
Async XLA Ops:
  0.6 4.4 %copy-start.5 = (bf16[1,8,2,49,256]{4,2,3,1,0:T(2,128)(2,1)S(1)}, bf16[1,8,2,49,256]{4,2,3,1,0:T(2,128)(2,1)}, u32[]{:S(2)}) copy-start(bf16[1,8,2,49,256]{4,2,3,1,0:T(2,128)(2,1)} %param.17) | copy-start | bytes 1204228
  0.6 4.4 %copy-start.6 = (bf16[1,8,2,49,256]{4,2,3,1,0:T(2,128)(2,1)S(1)}, bf16[1,8,2,49,256]{4,2,3,1,0:T(2,128)(2,1)}, u32[]{:S(2)}) copy-start(bf16[1,8,2,49,256]{4,2,3,1,0:T(2,128)(2,1)} %param.9) | copy-start | bytes 1204228
  2.4 13.1 %copy-start.7 = (f32[768]{0:T(1024)S(1)}, f32[768]{0:T(1024)}, u32[]{:S(2)}) copy-start(f32[768]{0:T(1024)} %param.14) | copy-start | bytes 9220
  2.4 13.1 %copy-start = (f32[256,768]{1,0:T(8,128)S(1)}, f32[256,768]{1,0:T(8,128)}, u32[]{:S(2)}) copy-start(f32[256,768]{1,0:T(8,128)} %w32.3) | copy-start | bytes 2359300
  2.4 13.1 %copy-start.1 = (f32[256,256]{1,0:T(8,128)S(1)}, f32[256,256]{1,0:T(8,128)}, u32[]{:S(2)}) copy-start(f32[256,256]{1,0:T(8,128)} %wp32.3) | copy-start | bytes 786436
  2.4 13.1 %copy-start.2 = (f32[256]{0:T(256)S(1)}, f32[256]{0:T(256)}, u32[]{:S(2)}) copy-start(f32[256]{0:T(256)} %param.11) | copy-start | bytes 3076
  2.4 13.1 %copy-start.3 = (f32[256]{0:T(256)S(1)}, f32[256]{0:T(256)}, u32[]{:S(2)}) copy-start(f32[256]{0:T(256)} %param.12) | copy-start | bytes 3076
  2.4 13.1 %copy-start.4 = (f32[256]{0:T(256)S(1)}, f32[256]{0:T(256)}, u32[]{:S(2)}) copy-start(f32[256]{0:T(256)} %param.16) | copy-start | bytes 3076
  2.5 13.1 %collective-permute-start = (bf16[2,4,49,256]{3,2,1,0:T(8,128)(2,1)S(1)}, bf16[2,4,49,256]{3,2,1,0:T(8,128)(2,1)S(1)}, u32[]{:S(2)}, u32[]{:S(2)}) collective-permute-start(bf16[2,4,49,256]{3,2,1,0:T(8,128)(2,1)S(1)} %pad_maximum_fusion), channel_id=1, source_target_pairs={{0,4},{4,0},{8,12},{12,8},{16,20},{20,16},{24,28},{28,24},{32,36},... | collective-permute-start | bytes 602120 | tf_op jit(solution)/shard_map/ppermute | solution.py:24
  5.2 19.7 %collective-permute-start.1 = (bf16[2,4,49,256]{3,2,1,0:T(8,128)(2,1)S(1)}, bf16[2,4,49,256]{3,2,1,0:T(8,128)(2,1)S(1)}, u32[]{:S(2)}, u32[]{:S(2)}) collective-permute-start(bf16[2,4,49,256]{3,2,1,0:T(8,128)(2,1)S(1)} %pick.1), channel_id=1, source_target_pairs={{0,252},{4,8},{8,4},{12,16},{16,12},{20,24},{24,20},{28,32},{32,28... | collective-permute-start | bytes 602120 | tf_op jit(solution)/shard_map/ppermute | solution.py:24
  24.6 9.3 %collective-permute-start.2 = (bf16[2,4,49,256]{3,2,1,0:T(8,128)(2,1)S(1)}, bf16[2,4,49,256]{3,2,1,0:T(8,128)(2,1)S(1)}, u32[]{:S(2)}, u32[]{:S(2)}) collective-permute-start(bf16[2,4,49,256]{3,2,1,0:T(8,128)(2,1)S(1)} %get-tuple-element.30), channel_id=1, source_target_pairs={{0,4},{4,0},{8,12},{12,8},{16,20},{20,16},{24,28},{28,24},{32,36},... | collective-permute-start | bytes 602120 | tf_op jit(solution)/shard_map/ppermute | solution.py:24
  51.5 15.3 %all-to-all-start.1 = ((bf16[8,72,128]{2,1,0:T(8,128)(2,1)}), bf16[8,72,128]{2,1,0:T(8,128)(2,1)S(1)}, u32[]{:S(2)}, u32[]{:S(2)}) async-start(bf16[8,72,128]{2,1,0:T(8,128)(2,1)} %spread.2), calls=%async_computation.1 | async-start | bytes 294912 | tf_op jit(solution)/shard_map/all_to_all | solution.py:251
  58.8 15.0 %collective-permute-start.3 = (bf16[2,4,49,256]{3,2,1,0:T(8,128)(2,1)S(1)}, bf16[2,4,49,256]{3,2,1,0:T(8,128)(2,1)S(1)}, u32[]{:S(2)}, u32[]{:S(2)}) collective-permute-start(bf16[2,4,49,256]{3,2,1,0:T(8,128)(2,1)S(1)} %get-tuple-element.34), channel_id=1, source_target_pairs={{0,252},{4,8},{8,4},{12,16},{16,12},{20,24},{24,20},{28,32},{32,28... | collective-permute-start | bytes 602120 | tf_op jit(solution)/shard_map/ppermute | solution.py:24
  67.6 18.3 %all-to-all-start.2 = ((bf16[32,72,128]{2,1,0:T(8,128)(2,1)}), bf16[32,72,128]{2,1,0:T(8,128)(2,1)S(1)}, u32[]{:S(2)}, u32[]{:S(2)}) async-start(bf16[32,72,128]{2,1,0:T(8,128)(2,1)} %spread.3), calls=%async_computation.2 | async-start | bytes 1179648 | tf_op jit(solution)/shard_map/all_to_all | solution.py:251

commit v4 on v3

--- a/solution.py
+++ b/solution.py
@@ -50,6 +50,7 @@
     else:
         mixed, gtok, send, acc_out = refs[:4]
     xs, gs, normT, gN, qkvT, doT, attT, dqT, acc, ext, w, wp = refs[-12:]
+    acc = acc if last else acc_out
     w[...] = w32[...].astype(bf16)
     wp[...] = wp32[...].astype(bf16)
     patch, width = tok.shape[2:]
@@ -176,9 +177,7 @@
             gtok[k] = (g_u + d_u.astype(f32)).astype(bf16)
         else:
             send[1, k] = d_u
-    if not last:
-        acc_out[...] = acc[...]
-    else:
+    if last:
         chunks, deep, lanes = pay.shape
         across = 4 * width // lanes
         for c in range(chunks):
@@ -228,14 +227,21 @@
     chunks, deep, lanes = got.shape
     across = 4 * width // lanes
     for c in range(chunks):
-        r, k = c // across, c % across
-        full[r * deep : (r + 1) * deep, k * lanes : (k + 1) * lanes] = got[c].astype(f32)
-    dwq[...] = full[:width, : 3 * width]
-    dwp[...] = full[:width, 3 * width :]
-    dbq[...] = full[width, : 3 * width]
-    dbp[...] = full[width, 3 * width :]
-    dgain[...] = full[width + EXT, :width]
-    dnb[...] = full[width + EXT, width : 2 * width]
+        top, k = c // across * deep, c % across
+        block = got[c].astype(f32)
+        n = min(deep, width - top)
+        cols = slice(k * lanes, (k + 1) * lanes)
+        if k * lanes < 3 * width:
+            dwq[top : top + n, cols] = block[:n]
+        else:
+            dwp[top : top + n, k * lanes - 3 * width : (k + 1) * lanes - 3 * width] = block[:n]
+        for m, row in enumerate((width, width + EXT)):
+            if top <= row < top + deep:
+                full[m : m + 1, cols] = block[row - top : row - top + 1]
+    dbq[...] = full[0, : 3 * width]
+    dbp[...] = full[0, 3 * width :]
+    dgain[...] = full[1, :width]
+    dnb[...] = full[1, width : 2 * width]
 
 
 def groups_of(bits, devices):
@@ -358,7 +364,7 @@
         ),
         in_specs=[vmem],
         out_specs=(vmem,) * 6,
-        scratch_shapes=[pltpu.VMEM((width + 2 * EXT, 4 * width), f32)],
+        scratch_shapes=[pltpu.VMEM((2, 4 * width), f32)],
         compiler_params=pltpu.CompilerParams(vmem_limit_bytes=16 << 20),
     )(got)
     return (mixed[None], gtok[None], dgain, dnb, dwq, dbq, dwp, dbp)

time: 87.4 us -> 87.4 us (level)
  no operation moved by 1% of the time
where the time goes in v4:
time: 87.4 us; the launch traced here: 87 us
  starting transfers between devices  29.6 us (34%)
  Pallas kernels  20.8 us (24%)
  blocking collectives  16.9 us (19%)
  waiting for transfers between devices  14.2 us (16%)
  local copies, waits for them, and re-layouts  3.95 us (5%)
  between operations  1.54 us (2%)
    pallas_call x2, Pallas kernels, block(): pl.pallas_call(functools.partial(block_kernel, frame_total, last), name='...  18 us
    all_to_all x1, blocking collectives, exchange(): lax.all_to_all(x, AXES, 0, 0, tiled=True, axis_index_groups=groups_of(bit...  16.9 us
    ppermute x4, starting transfers between devices, swapped(): return lax.ppermute(array, 'frame', pairs)  16.3 us
    all_to_all x2, waiting for transfers between devices, exchange(): lax.all_to_all(x, AXES, 0, 0, tiled=True, axis_index_groups=groups_of(bit...  14.2 us
    all_to_all x2, starting transfers between devices, exchange(): lax.all_to_all(x, AXES, 0, 0, tiled=True, axis_index_groups=groups_of(bit...  13.4 us
    unnamed x18, local copies, waits for them, and re-layouts  2.17 us
  transfers between devices with their start and end apart: 6, of which 2 were waited for; matrix products, arithmetic and copies ran while one was open for 3% of the time, Pallas kernels for 22%

profile of v4, /device:TPU:1, one launch (start us, length us, event | category | flops | bytes accessed | tf_op | source)
XLA Modules:
  0.0 87.0 jit_solution(12701661962237259836)
XLA Ops:
  0.6 0.0 copy-start.5
  0.6 0.0 copy-start.6
  0.7 1.5 %constant_dynamic-slice_fusion = (bf16[1,4,1,49,256]{4,2,3,1,0:T(2,128)(2,1)S(1)}, bf16[1,4,1,49,256]{4,2,3,1,0:T(2,128)(2,1)S(1)}) fusion(bf16[1,8,2,49,256]{4,2,3,1,0:T(2,128)(2,1)} %param.17, s32[]{:T(128)S(6)} %select_n.13, s32[]{:T(128)S(6)} %select_n.15, bf16[1,8,2,49,256]{4,2,3,1,0:T(2,128)(2,1)} %param.9), kind=kLoop, calls=%fused_computation.5 | loop fusion | bytes 401416 | tf_op jit(solution)/shard_map/dynamic_slice | solution.py:283
  2.2 0.1 copy.33
  2.3 0.1 copy.34
  2.4 0.0 copy-start.7
  2.4 0.0 copy-start
  2.4 0.0 copy-start.1
  2.4 0.0 copy-start.2
  2.4 0.0 copy-start.3
  2.4 0.0 copy-start.4
  2.5 2.6 %collective-permute-start = (bf16[2,4,49,256]{3,2,1,0:T(8,128)(2,1)S(1)}, bf16[2,4,49,256]{3,2,1,0:T(8,128)(2,1)S(1)}, u32[]{:S(2)}, u32[]{:S(2)}) collective-permute-start(bf16[2,4,49,256]{3,2,1,0:T(8,128)(2,1)S(1)} %pad_maximum_fusion), channel_id=1, source_target_pairs={{0,4},{4,0},{8,12},{12,8},{16,20},{20,16},{24,28},{28,24},{32,36},... | collective-permute-start | bytes 602120 | tf_op jit(solution)/shard_map/ppermute | solution.py:24
  5.0 0.0 copy-done.5
  5.0 0.0 copy-done.6
  5.0 0.1 copy_bitcast_fusion
  5.2 9.7 %collective-permute-start.1 = (bf16[2,4,49,256]{3,2,1,0:T(8,128)(2,1)S(1)}, bf16[2,4,49,256]{3,2,1,0:T(8,128)(2,1)S(1)}, u32[]{:S(2)}, u32[]{:S(2)}) collective-permute-start(bf16[2,4,49,256]{3,2,1,0:T(8,128)(2,1)S(1)} %pick.1), channel_id=1, source_target_pairs={{0,252},{4,8},{8,4},{12,16},{16,12},{20,24},{24,20},{28,32},{32,28... | collective-permute-start | bytes 602120 | tf_op jit(solution)/shard_map/ppermute | solution.py:24
  15.5 0.0 copy-done.7
  15.5 0.0 collective-permute-done.halo
  15.5 0.0 copy-done
  15.5 0.0 copy-done.1
  15.6 0.0 copy-done.2
  15.6 0.0 copy-done.3
  15.6 0.0 copy-done.4
  15.6 9.0 %first_window.1 = (bf16[4,49,256]{2,1,0:T(8,128)(2,1)S(1)}, bf16[4,49,256]{2,1,0:T(8,128)(2,1)S(1)}, bf16[2,4,49,256]{3,2,1,0:T(8,128)(2,1)S(1)}, f32[288,1024]{1,0:T(8,128)S(1)}) custom-call(s32[1]{0:T(128)S(6)} %copy.35.lengths, bf16[8,2,49,256]{3,2,1,0:T(8,128)(2,1)S(1)} %get-tuple-element.63.tok, bf16[8,2,49,256]{3,2,1,0:T(8,128)(2,1)S(1)} %get-tuple-element.62.gr, ...), custom_call_target="tpu_custom_call" | custom-call | flops 8000000000 | bytes 8000000 | tf_op jit(solution)/shard_map/first_window/pallas_call | solution.py:302
  24.6 0.3 collective-permute-start.2
  24.9 0.0 collective-permute-done.1.halo
  24.9 9.0 %second_window.1 = (bf16[4,49,256]{2,1,0:T(8,128)(2,1)S(1)}, bf16[4,49,256]{2,1,0:T(8,128)(2,1)S(1)}, bf16[2,4,49,256]{3,2,1,0:T(8,128)(2,1)S(1)}, bf16[32,72,128]{2,1,0:T(8,128)(2,1)S(1)}) custom-call(s32[1]{0:T(128)S(6)} %copy.35.lengths, bf16[8,2,49,256]{3,2,1,0:T(8,128)(2,1)S(1)} %get-tuple-element.63.tok, ...), custom_call_target="tpu_custom_call" | custom-call | flops 8000000000 | bytes 8000000 | tf_op jit(solution)/shard_map/second_window/pallas_call | solution.py:302
  33.9 0.0 collective-permute-done.2.back1
  33.9 16.9 %all_to_all.15.parts = bf16[32,72,128]{2,1,0:T(8,128)(2,1)S(1)} all-to-all(bf16[32,72,128]{2,1,0:T(8,128)(2,1)S(1)} %get-tuple-element.37), channel_id=1, replica_groups={{0,1,2,3,32,33,34,35,64,65,66,67,96,97,98,99,128,129,130,131,160,161,16..., dimensions={0} | all-to-all | bytes 1179648 | tf_op jit(solution)/shard_map/all_to_all | solution.py:257
  50.7 0.8 spread.2
  51.5 7.3 %all-to-all-start.1 = ((bf16[8,72,128]{2,1,0:T(8,128)(2,1)}), bf16[8,72,128]{2,1,0:T(8,128)(2,1)S(1)}, u32[]{:S(2)}, u32[]{:S(2)}) async-start(bf16[8,72,128]{2,1,0:T(8,128)(2,1)} %spread.2), calls=%async_computation.1 | async-start | bytes 294912 | tf_op jit(solution)/shard_map/all_to_all | solution.py:257
  58.8 3.8 %collective-permute-start.3 = (bf16[2,4,49,256]{3,2,1,0:T(8,128)(2,1)S(1)}, bf16[2,4,49,256]{3,2,1,0:T(8,128)(2,1)S(1)}, u32[]{:S(2)}, u32[]{:S(2)}) collective-permute-start(bf16[2,4,49,256]{3,2,1,0:T(8,128)(2,1)S(1)} %get-tuple-element.34), channel_id=1, source_target_pairs={{0,252},{4,8},{8,4},{12,16},{16,12},{20,24},{24,20},{28,32},{32,28... | collective-permute-start | bytes 602120 | tf_op jit(solution)/shard_map/ppermute | solution.py:24
  62.5 4.2 %all-to-all-done.1.parts = bf16[8,72,128]{2,1,0:T(8,128)(2,1)S(1)} async-done(((bf16[8,72,128]{2,1,0:T(8,128)(2,1)}), bf16[8,72,128]{2,1,0:T(8,128)(2,1)S(1)}, u32[]{:S(2)}, u32[]{:S(2)}) %all-to-all-start.1) | async-done | bytes 147488 | tf_op jit(solution)/shard_map/all_to_all | solution.py:257
  66.8 0.9 spread.3
  67.6 6.1 %all-to-all-start.2 = ((bf16[32,72,128]{2,1,0:T(8,128)(2,1)}), bf16[32,72,128]{2,1,0:T(8,128)(2,1)S(1)}, u32[]{:S(2)}, u32[]{:S(2)}) async-start(bf16[32,72,128]{2,1,0:T(8,128)(2,1)} %spread.3), calls=%async_computation.2 | async-start | bytes 1179648 | tf_op jit(solution)/shard_map/all_to_all | solution.py:257
  73.7 0.0 collective-permute-done.3.back2
  73.7 0.1 join.1
  73.9 1.1 %copy.27 = bf16[1,8,2,49,256]{4,2,3,1,0:T(2,128)(2,1)} copy(bf16[1,8,2,49,256]{4,3,2,1,0:T(8,128)(2,1)S(1)} %bitcast.16) | data formatting | bytes 802816
  75.0 1.1 %copy.28 = bf16[1,8,2,49,256]{4,2,3,1,0:T(2,128)(2,1)} copy(bf16[1,8,2,49,256]{4,3,2,1,0:T(8,128)(2,1)S(1)} %bitcast.15) | data formatting | bytes 802816
  76.0 10.0 %all-to-all-done.2.got = bf16[32,72,128]{2,1,0:T(8,128)(2,1)S(1)} async-done(((bf16[32,72,128]{2,1,0:T(8,128)(2,1)}), bf16[32,72,128]{2,1,0:T(8,128)(2,1)S(1)}, u32[]{:S(2)}, u32[]{:S(2)}) %all-to-all-start.2) | async-done | bytes 589856 | tf_op jit(solution)/shard_map/all_to_all | solution.py:257
  86.0 1.0 %unpack.1 = (f32[256]{0:T(256)}, f32[256]{0:T(256)}, f32[256,768]{1,0:T(8,128)}, f32[768]{0:T(1024)}, f32[256,256]{1,0:T(8,128)}, /*index=5*/f32[256]{0:T(256)}) custom-call(bf16[32,72,128]{2,1,0:T(8,128)(2,1)S(1)} %all-to-all-done.2.got), custom_call_target="tpu_custom_call" | custom-call | tf_op jit(solution)/shard_map/unpack/pallas_call | solution.py:354
  (5 shorter events, 0.1 us)
Async XLA Ops:
  0.6 4.4 %copy-start.5 = (bf16[1,8,2,49,256]{4,2,3,1,0:T(2,128)(2,1)S(1)}, bf16[1,8,2,49,256]{4,2,3,1,0:T(2,128)(2,1)}, u32[]{:S(2)}) copy-start(bf16[1,8,2,49,256]{4,2,3,1,0:T(2,128)(2,1)} %param.17) | copy-start | bytes 1204228
  0.6 4.4 %copy-start.6 = (bf16[1,8,2,49,256]{4,2,3,1,0:T(2,128)(2,1)S(1)}, bf16[1,8,2,49,256]{4,2,3,1,0:T(2,128)(2,1)}, u32[]{:S(2)}) copy-start(bf16[1,8,2,49,256]{4,2,3,1,0:T(2,128)(2,1)} %param.9) | copy-start | bytes 1204228
  2.4 13.1 %copy-start.7 = (f32[768]{0:T(1024)S(1)}, f32[768]{0:T(1024)}, u32[]{:S(2)}) copy-start(f32[768]{0:T(1024)} %param.14) | copy-start | bytes 9220
  2.4 13.1 %copy-start = (f32[256,768]{1,0:T(8,128)S(1)}, f32[256,768]{1,0:T(8,128)}, u32[]{:S(2)}) copy-start(f32[256,768]{1,0:T(8,128)} %w32.3) | copy-start | bytes 2359300
  2.4 13.1 %copy-start.1 = (f32[256,256]{1,0:T(8,128)S(1)}, f32[256,256]{1,0:T(8,128)}, u32[]{:S(2)}) copy-start(f32[256,256]{1,0:T(8,128)} %wp32.3) | copy-start | bytes 786436
  2.4 13.1 %copy-start.2 = (f32[256]{0:T(256)S(1)}, f32[256]{0:T(256)}, u32[]{:S(2)}) copy-start(f32[256]{0:T(256)} %param.11) | copy-start | bytes 3076
  2.4 13.1 %copy-start.3 = (f32[256]{0:T(256)S(1)}, f32[256]{0:T(256)}, u32[]{:S(2)}) copy-start(f32[256]{0:T(256)} %param.12) | copy-start | bytes 3076
  2.4 13.1 %copy-start.4 = (f32[256]{0:T(256)S(1)}, f32[256]{0:T(256)}, u32[]{:S(2)}) copy-start(f32[256]{0:T(256)} %param.16) | copy-start | bytes 3076
  2.5 13.1 %collective-permute-start = (bf16[2,4,49,256]{3,2,1,0:T(8,128)(2,1)S(1)}, bf16[2,4,49,256]{3,2,1,0:T(8,128)(2,1)S(1)}, u32[]{:S(2)}, u32[]{:S(2)}) collective-permute-start(bf16[2,4,49,256]{3,2,1,0:T(8,128)(2,1)S(1)} %pad_maximum_fusion), channel_id=1, source_target_pairs={{0,4},{4,0},{8,12},{12,8},{16,20},{20,16},{24,28},{28,24},{32,36},... | collective-permute-start | bytes 602120 | tf_op jit(solution)/shard_map/ppermute | solution.py:24
  5.2 19.7 %collective-permute-start.1 = (bf16[2,4,49,256]{3,2,1,0:T(8,128)(2,1)S(1)}, bf16[2,4,49,256]{3,2,1,0:T(8,128)(2,1)S(1)}, u32[]{:S(2)}, u32[]{:S(2)}) collective-permute-start(bf16[2,4,49,256]{3,2,1,0:T(8,128)(2,1)S(1)} %pick.1), channel_id=1, source_target_pairs={{0,252},{4,8},{8,4},{12,16},{16,12},{20,24},{24,20},{28,32},{32,28... | collective-permute-start | bytes 602120 | tf_op jit(solution)/shard_map/ppermute | solution.py:24
  24.6 9.3 %collective-permute-start.2 = (bf16[2,4,49,256]{3,2,1,0:T(8,128)(2,1)S(1)}, bf16[2,4,49,256]{3,2,1,0:T(8,128)(2,1)S(1)}, u32[]{:S(2)}, u32[]{:S(2)}) collective-permute-start(bf16[2,4,49,256]{3,2,1,0:T(8,128)(2,1)S(1)} %get-tuple-element.30), channel_id=1, source_target_pairs={{0,4},{4,0},{8,12},{12,8},{16,20},{20,16},{24,28},{28,24},{32,36},... | collective-permute-start | bytes 602120 | tf_op jit(solution)/shard_map/ppermute | solution.py:24
  51.5 15.3 %all-to-all-start.1 = ((bf16[8,72,128]{2,1,0:T(8,128)(2,1)}), bf16[8,72,128]{2,1,0:T(8,128)(2,1)S(1)}, u32[]{:S(2)}, u32[]{:S(2)}) async-start(bf16[8,72,128]{2,1,0:T(8,128)(2,1)} %spread.2), calls=%async_computation.1 | async-start | bytes 294912 | tf_op jit(solution)/shard_map/all_to_all | solution.py:257
  58.8 15.0 %collective-permute-start.3 = (bf16[2,4,49,256]{3,2,1,0:T(8,128)(2,1)S(1)}, bf16[2,4,49,256]{3,2,1,0:T(8,128)(2,1)S(1)}, u32[]{:S(2)}, u32[]{:S(2)}) collective-permute-start(bf16[2,4,49,256]{3,2,1,0:T(8,128)(2,1)S(1)} %get-tuple-element.34), channel_id=1, source_target_pairs={{0,252},{4,8},{8,4},{12,16},{16,12},{20,24},{24,20},{28,32},{32,28... | collective-permute-start | bytes 602120 | tf_op jit(solution)/shard_map/ppermute | solution.py:24
  67.6 18.3 %all-to-all-start.2 = ((bf16[32,72,128]{2,1,0:T(8,128)(2,1)}), bf16[32,72,128]{2,1,0:T(8,128)(2,1)S(1)}, u32[]{:S(2)}, u32[]{:S(2)}) async-start(bf16[32,72,128]{2,1,0:T(8,128)(2,1)} %spread.3), calls=%async_computation.2 | async-start | bytes 1179648 | tf_op jit(solution)/shard_map/all_to_all | solution.py:257
